TPU v7x, 32 devices: a whole 2x2x4 slice. The times are simulated.
32 devices in a mesh: ctx: 8 (over z, x), heads: 4 (over y, core).
Axes of the slice: x: 2, y: 2, z: 4, core: 2. Of those that a mesh axis runs over, the one named last changes fastest.
Arguments:
- tokens: bfloat16 [4096, 1024], P(('ctx', 'heads')), may hold values from -6 to 6
- d_out: bfloat16 [4096, 1024], P(('ctx', 'heads')), may hold values from -6 to 6
- segment_ids: int32 [4096], P(('ctx', 'heads')), may hold values from 0 to 2, as said below
- position_ids: int32 [4096], P(('ctx', 'heads')), may hold values from 0 to 2047, as said below
- w_qkv: bfloat16 [1024, 3072], P('ctx'), may hold values from -0.1875 to 0.1875
- w_attn: bfloat16 [1024, 1024], P('ctx'), may hold values from -1.5 to 1.5
- w_in: bfloat16 [1024, 5248], P('ctx'), may hold values from -0.1875 to 0.1875
- w_out: bfloat16 [2624, 1024], P(None, 'ctx'), may hold values from -0.25 to 0.25
- gain_attn: bfloat16 [1024], P('ctx'), may hold values from 0.25 to 1.75
- gain_mlp: bfloat16 [1024], P('ctx'), may hold values from 0.25 to 1.75
Outputs:
- out: bfloat16 [4096, 1024], P(('ctx', 'heads'))
- grad_input: float32 [4096, 1024], P(('ctx', 'heads'))
- grad_w_qkv: float32 [1024, 3072], P('ctx')
- grad_w_attn: float32 [1024, 1024], P('ctx')
- grad_w_in: float32 [1024, 5248], P('ctx')
- grad_w_out: float32 [2624, 1024], P(None, 'ctx')
- grad_gain_attn: float32 [1024], P('ctx')
- grad_gain_mlp: float32 [1024], P('ctx')
Inputs may be any that keep to these rules, and one draw needn't show every extreme that they name: `segment_ids`: starts at 0 and rises by 0 or 1 from one token to the next. The tokens fall into aligned blocks of 2048; one block, at a drawn place, is one sequence of exactly 2048 tokens, every other block holds two sequences split at a drawn point, each of 512 tokens or more. `position_ids`: the number of earlier tokens with the same segment id.
All inputs are finite; a program needn't handle non-finite values.
Results may differ from a plain program's by a relative error of at most 0.02.
Values may be sent and summed in bfloat16 or wider, within the bound.
A program may use at most 192 MiB of HBM per device.

v0:
```python
import jax
import jax.numpy as jnp
from jax import lax
from jax.sharding import PartitionSpec as P

H = 16
HD = 64
FF = 2624
SEQ_MAX = 2048


NEG_FILL = -1e30


def passed_along(value, axis, steps):
    count = lax.axis_size(axis)
    initial, last = (max(0, -steps), min(count, count - steps))
    return lax.ppermute(value, axis, [(source, source + steps) for source in range(initial, last)])


def layer_norm(values, scale_gain):
    average = jnp.mean(values, axis=-1, keepdims=True)
    centred = values - average
    inverse_std = lax.rsqrt(jnp.mean(centred * centred, axis=-1, keepdims=True) + 1e-05)
    normed = centred * inverse_std
    return (normed * scale_gain, normed, inverse_std)


def norm_back(upstream, normed, inverse_std, scale_gain):
    scaled = upstream * scale_gain
    inner_term = (
        scaled
        - jnp.mean(scaled, axis=-1, keepdims=True)
        - normed * jnp.mean(scaled * normed, axis=-1, keepdims=True)
    )
    return (inner_term * inverse_std, jnp.sum(upstream * normed, axis=0))


def rope_tables(positions, head_dim):
    half_dim = head_dim // 2
    freqs = jnp.power(160000.0, -(2.0 * jnp.arange(half_dim, dtype=jnp.float32)) / head_dim)
    angles = positions.astype(jnp.float32)[:, None] * freqs[None, :]
    cosine = jnp.concatenate([jnp.cos(angles), jnp.cos(angles)], axis=-1)[:, None, :]
    sine = jnp.concatenate([jnp.sin(angles), jnp.sin(angles)], axis=-1)[:, None, :]
    return (cosine, sine)


def rotate(values, cosine, sine):
    half_dim = values.shape[-1] // 2
    turned = jnp.concatenate([-values[..., half_dim:], values[..., :half_dim]], axis=-1)
    return values * cosine + turned * sine


def rotate_back(upstream, cosine, sine):
    half_dim = upstream.shape[-1] // 2
    weighted = upstream * sine
    turned = jnp.concatenate([weighted[..., half_dim:], -weighted[..., :half_dim]], axis=-1)
    return upstream * cosine + turned


def body(tokens, d_out, segment_ids, position_ids, w_qkv, w_attn, w_in, w_out, gain_attn, gain_mlp):
    full_qkv, full_attn, full_in, full_out, gain_one, gain_two = (
        lax.all_gather(w_qkv, "ctx", axis=0, tiled=True),
        lax.all_gather(w_attn, "ctx", axis=0, tiled=True),
        lax.all_gather(w_in, "ctx", axis=0, tiled=True),
        lax.all_gather(w_out, "ctx", axis=1, tiled=True),
        lax.all_gather(gain_attn, "ctx", axis=0, tiled=True),
        lax.all_gather(gain_mlp, "ctx", axis=0, tiled=True),
    )
    gain_one = gain_one.astype(jnp.float32)
    gain_two = gain_two.astype(jnp.float32)
    row_count, model_width = tokens.shape
    groups = lax.axis_size("heads")
    per_group = H // groups
    lane_width = per_group * HD
    block_rows = row_count * groups
    tile_rows = min(512, block_rows)
    tile_count = block_rows // tile_rows
    cosine, sine = rope_tables(position_ids, HD)
    residual_in = tokens.astype(jnp.float32)
    normed_attn, plain_one, inverse_one = layer_norm(residual_in, gain_one)
    attn_input = normed_attn.astype(jnp.bfloat16)
    projected = jnp.dot(attn_input, full_qkv, preferred_element_type=jnp.float32).reshape(
        row_count, 3, H, HD
    )
    rotated = jnp.stack(
        [
            rotate(projected[:, 0], cosine, sine),
            rotate(projected[:, 1], cosine, sine),
            projected[:, 2],
        ],
        axis=1,
    )
    outgoing = rotated.astype(jnp.bfloat16).reshape(row_count, 3, groups, lane_width)
    seg_marks = jnp.broadcast_to((segment_ids + 1)[:, None, None], (row_count, 1, groups))
    grouped, block_marks = (
        lax.all_to_all(outgoing, "heads", split_axis=2, concat_axis=0, tiled=True),
        lax.all_to_all(seg_marks, "heads", split_axis=2, concat_axis=0, tiled=True),
    )
    queries = grouped[:, 0, 0].reshape(block_rows, per_group, HD)
    own_kv = grouped[:, 1:, 0]
    own_marks = block_marks[:, 0, 0]
    reach_blocks = (SEQ_MAX + block_rows - 2) // block_rows
    offsets = [0]
    for distance in range(1, reach_blocks + 1):
        offsets = offsets + [distance, -distance]
    kv_list = [own_kv]
    mark_list = [own_marks]
    for offset in offsets[1:]:
        got_kv, got_marks = passed_along((own_kv, own_marks), "ctx", offset)
        kv_list.append(got_kv)
        mark_list.append(got_marks)
    stack_kv = jnp.stack(kv_list)
    stack_marks = jnp.stack(mark_list)
    block_count = stack_kv.shape[0]

    def tile_scores(query_tile, query_marks, kv_tile, key_marks):
        key_tile = kv_tile[:, 0].reshape(tile_rows, per_group, HD)
        raw = (
            jnp.einsum("qhd,khd->hqk", query_tile, key_tile, preferred_element_type=jnp.float32)
            * 0.125
        )
        allowed = (query_marks[:, None] == key_marks[None, :])[None]
        return (jnp.where(allowed, raw, NEG_FILL), allowed)

    def meets(query_marks, key_marks):
        return jnp.logical_and(query_marks[0] <= key_marks[-1], key_marks[0] <= query_marks[-1])

    def sweep(query_pos, update, initial):
        start = query_pos * tile_rows
        query_tile = lax.dynamic_slice_in_dim(queries, start, tile_rows, 0)
        query_marks = lax.dynamic_slice_in_dim(own_marks, start, tile_rows, 0)

        def sweep_visit(flat, loop_carry):
            which = flat // tile_count
            key_start = flat % tile_count * tile_rows
            kv_tile = lax.dynamic_slice_in_dim(stack_kv[which], key_start, tile_rows, 0)
            key_marks = lax.dynamic_slice_in_dim(stack_marks[which], key_start, tile_rows, 0)
            return lax.cond(
                meets(query_marks, key_marks),
                lambda inner: update(inner, query_tile, query_marks, kv_tile, key_marks),
                lambda inner: inner,
                loop_carry,
            )

        return lax.fori_loop(0, block_count * tile_count, sweep_visit, initial)

    def log_norm_tile(query_pos):

        def update(loop_carry, query_tile, query_marks, kv_tile, key_marks):
            running_max, running_sum = loop_carry
            scores, allowed = tile_scores(query_tile, query_marks, kv_tile, key_marks)
            new_max = jnp.maximum(running_max, jnp.max(scores, axis=-1))
            shifted = jnp.where(allowed, jnp.exp(scores - new_max[..., None]), 0.0)
            return (
                new_max,
                running_sum * jnp.exp(running_max - new_max) + jnp.sum(shifted, axis=-1),
            )

        start_max = jnp.full((per_group, tile_rows), NEG_FILL, jnp.float32)
        running_max, running_sum = sweep(query_pos, update, (start_max, jnp.zeros_like(start_max)))
        return running_max + jnp.log(running_sum)

    log_norm = lax.map(log_norm_tile, jnp.arange(tile_count))
    log_norm_flat = log_norm.transpose(1, 0, 2).reshape(per_group, block_rows)

    def attend_tile(query_pos):
        norm_q = log_norm[query_pos]

        def update(accumulated, query_tile, query_marks, kv_tile, key_marks):
            scores, allowed = tile_scores(query_tile, query_marks, kv_tile, key_marks)
            probability = jnp.where(allowed, jnp.exp(scores - norm_q[..., None]), 0.0).astype(
                jnp.bfloat16
            )
            value_tile = kv_tile[:, 1].reshape(tile_rows, per_group, HD)
            return accumulated + jnp.einsum(
                "hqk,khd->qhd", probability, value_tile, preferred_element_type=jnp.float32
            )

        return sweep(query_pos, update, jnp.zeros((tile_rows, per_group, HD), jnp.float32))

    attended = lax.map(attend_tile, jnp.arange(tile_count)).reshape(block_rows, per_group, HD)
    gathered = lax.all_to_all(
        attended.reshape(block_rows, lane_width).astype(jnp.bfloat16),
        "heads",
        split_axis=0,
        concat_axis=1,
        tiled=True,
    )
    middle = residual_in + jnp.dot(gathered, full_attn, preferred_element_type=jnp.float32)
    normed_mlp, plain_two, inverse_two = layer_norm(middle, gain_two)
    mlp_input = normed_mlp.astype(jnp.bfloat16)
    gate_up = jnp.dot(mlp_input, full_in, preferred_element_type=jnp.float32)
    gate_left = gate_up[:, :FF]
    gate_right = gate_up[:, FF:]
    mixed = (jax.nn.gelu(gate_left, approximate=False) * gate_right).astype(jnp.bfloat16)
    result = (middle + jnp.dot(mixed, full_out, preferred_element_type=jnp.float32)).astype(
        jnp.bfloat16
    )
    grad_w_out = jnp.einsum("tf,td->fd", mixed, d_out, preferred_element_type=jnp.float32)
    grad_mixed = jnp.einsum("td,fd->tf", d_out, full_out, preferred_element_type=jnp.float32)
    _, pull_gate = jax.vjp(
        lambda left_in, right_in: jax.nn.gelu(left_in, approximate=False) * right_in,
        gate_left,
        gate_right,
    )
    grad_left, grad_right = pull_gate(grad_mixed)
    grad_gate_up = jnp.concatenate([grad_left, grad_right], axis=1).astype(jnp.bfloat16)
    grad_w_in = jnp.einsum("td,tf->df", mlp_input, grad_gate_up, preferred_element_type=jnp.float32)
    grad_mlp_input = jnp.einsum(
        "tf,df->td", grad_gate_up, full_in, preferred_element_type=jnp.float32
    )
    grad_norm_mid, grad_gain_two = norm_back(grad_mlp_input, plain_two, inverse_two, gain_two)
    grad_middle = d_out.astype(jnp.float32) + grad_norm_mid
    grad_branch = grad_middle.astype(jnp.bfloat16)
    grad_w_attn = jnp.einsum("td,te->de", gathered, grad_branch, preferred_element_type=jnp.float32)
    grad_gathered = jnp.einsum(
        "te,de->td", grad_branch, full_attn, preferred_element_type=jnp.float32
    ).astype(jnp.bfloat16)
    grad_heads_in = lax.all_to_all(grad_gathered, "heads", split_axis=1, concat_axis=0, tiled=True)
    grad_out = grad_heads_in.reshape(block_rows, per_group, HD)
    row_delta = jnp.sum(grad_out.astype(jnp.float32) * attended, axis=-1).T

    def block_back(which, grad_query):

        def block_visit(flat, loop_state):
            query_start = flat // tile_count * tile_rows
            key_start = flat % tile_count * tile_rows
            query_tile = lax.dynamic_slice_in_dim(queries, query_start, tile_rows, 0)
            query_marks = lax.dynamic_slice_in_dim(own_marks, query_start, tile_rows, 0)
            out_tile = lax.dynamic_slice_in_dim(grad_out, query_start, tile_rows, 0)
            kv_tile = lax.dynamic_slice_in_dim(stack_kv[which], key_start, tile_rows, 0)
            key_marks = lax.dynamic_slice_in_dim(stack_marks[which], key_start, tile_rows, 0)

            def compute_tile(inner):
                grad_q_acc, grad_kv_acc = inner
                scores, allowed = tile_scores(query_tile, query_marks, kv_tile, key_marks)
                norm_q = lax.dynamic_slice_in_dim(log_norm_flat, query_start, tile_rows, 1)
                delta_q = lax.dynamic_slice_in_dim(row_delta, query_start, tile_rows, 1)
                probability = jnp.where(allowed, jnp.exp(scores - norm_q[..., None]), 0.0)
                key_tile = kv_tile[:, 0].reshape(tile_rows, per_group, HD)
                value_tile = kv_tile[:, 1].reshape(tile_rows, per_group, HD)
                grad_prob = jnp.einsum(
                    "qhd,khd->hqk", out_tile, value_tile, preferred_element_type=jnp.float32
                )
                grad_score = (probability * (grad_prob - delta_q[..., None])).astype(jnp.bfloat16)
                query_part = (
                    jnp.einsum(
                        "hqk,khd->qhd", grad_score, key_tile, preferred_element_type=jnp.float32
                    )
                    * 0.125
                )
                key_part = (
                    jnp.einsum(
                        "hqk,qhd->khd", grad_score, query_tile, preferred_element_type=jnp.float32
                    )
                    * 0.125
                )
                value_part = jnp.einsum(
                    "hqk,qhd->khd",
                    probability.astype(jnp.bfloat16),
                    out_tile,
                    preferred_element_type=jnp.float32,
                )
                grad_q_acc = lax.dynamic_update_slice_in_dim(
                    grad_q_acc,
                    lax.dynamic_slice_in_dim(grad_q_acc, query_start, tile_rows, 0) + query_part,
                    query_start,
                    0,
                )
                kv_part = jnp.stack(
                    [
                        key_part.reshape(tile_rows, lane_width),
                        value_part.reshape(tile_rows, lane_width),
                    ],
                    axis=1,
                )
                grad_kv_acc = lax.dynamic_update_slice_in_dim(
                    grad_kv_acc,
                    lax.dynamic_slice_in_dim(grad_kv_acc, key_start, tile_rows, 0) + kv_part,
                    key_start,
                    0,
                )
                return (grad_q_acc, grad_kv_acc)

            return lax.cond(
                meets(query_marks, key_marks), compute_tile, lambda inner: inner, loop_state
            )

        initial = (grad_query, jnp.zeros((block_rows, 2, lane_width), jnp.float32))
        return lax.fori_loop(0, tile_count * tile_count, block_visit, initial)

    grad_query, grad_kv = block_back(0, jnp.zeros((block_rows, per_group, HD), jnp.float32))
    for station in range(1, len(offsets)):
        grad_query, portion = block_back(station, grad_query)
        grad_kv = grad_kv + passed_along(
            portion.astype(jnp.bfloat16), "ctx", -offsets[station]
        ).astype(portion.dtype)
    combined = jnp.concatenate([grad_query.reshape(block_rows, 1, lane_width), grad_kv], axis=1)
    combined = combined.astype(jnp.bfloat16).reshape(block_rows, 3, 1, lane_width)
    returned = lax.all_to_all(combined, "heads", split_axis=0, concat_axis=2, tiled=True)
    returned = returned.reshape(row_count, 3, H, HD).astype(jnp.float32)
    unrotated = jnp.stack(
        [
            rotate_back(returned[:, 0], cosine, sine),
            rotate_back(returned[:, 1], cosine, sine),
            returned[:, 2],
        ],
        axis=1,
    )
    grad_projected = unrotated.reshape(row_count, 3 * model_width).astype(jnp.bfloat16)
    grad_w_qkv = jnp.einsum(
        "td,te->de", attn_input, grad_projected, preferred_element_type=jnp.float32
    )
    grad_attn_input = jnp.einsum(
        "te,de->td", grad_projected, full_qkv, preferred_element_type=jnp.float32
    )
    grad_norm_in, grad_gain_one = norm_back(grad_attn_input, plain_one, inverse_one, gain_one)
    grad_input = grad_middle + grad_norm_in
    reduced = (
        lax.psum_scatter(
            grad_w_qkv.astype(jnp.bfloat16), "ctx", scatter_dimension=0, tiled=True
        ).astype(jnp.float32),
        lax.psum_scatter(
            grad_w_attn.astype(jnp.bfloat16), "ctx", scatter_dimension=0, tiled=True
        ).astype(jnp.float32),
        lax.psum_scatter(
            grad_w_in.astype(jnp.bfloat16), "ctx", scatter_dimension=0, tiled=True
        ).astype(jnp.float32),
        lax.psum_scatter(
            grad_w_out.astype(jnp.bfloat16), "ctx", scatter_dimension=1, tiled=True
        ).astype(jnp.float32),
        lax.psum_scatter(
            grad_gain_one.astype(jnp.bfloat16), "ctx", scatter_dimension=0, tiled=True
        ).astype(jnp.float32),
        lax.psum_scatter(
            grad_gain_two.astype(jnp.bfloat16), "ctx", scatter_dimension=0, tiled=True
        ).astype(jnp.float32),
    )
    totals = (
        lax.psum(reduced[0].astype(jnp.bfloat16), "heads").astype(jnp.float32),
        lax.psum(reduced[1].astype(jnp.bfloat16), "heads").astype(jnp.float32),
        lax.psum(reduced[2].astype(jnp.bfloat16), "heads").astype(jnp.float32),
        lax.psum(reduced[3].astype(jnp.bfloat16), "heads").astype(jnp.float32),
        lax.psum(reduced[4].astype(jnp.bfloat16), "heads").astype(jnp.float32),
        lax.psum(reduced[5].astype(jnp.bfloat16), "heads").astype(jnp.float32),
    )
    sum_qkv, sum_attn, sum_in, sum_out, sum_gain_one, sum_gain_two = totals
    return (result, grad_input, sum_qkv, sum_attn, sum_in, sum_out, sum_gain_one, sum_gain_two)


def solution(mesh):
    return jax.shard_map(
        body,
        mesh=mesh,
        in_specs=(
            P(("ctx", "heads"), None),
            P(("ctx", "heads"), None),
            P(("ctx", "heads")),
            P(("ctx", "heads")),
            P("ctx", None),
            P("ctx", None),
            P("ctx", None),
            P(None, "ctx"),
            P("ctx"),
            P("ctx"),
        ),
        out_specs=(
            P(("ctx", "heads"), None),
            P(("ctx", "heads"), None),
            P("ctx", None),
            P("ctx", None),
            P("ctx", None),
            P(None, "ctx"),
            P("ctx"),
            P("ctx"),
        ),
        check_vma=False,
    )
```

profile of v0, /device:TPU:0, one launch (start us, length us, event | category | flops | bytes accessed | tf_op | source)
XLA Modules:
  0.0 1106.7 jit_solution(4634724985036654381)
XLA Ops:
  9.4 22.5 %all-gather = bf16[8,1,128]{2,1,0:T(2,128)(2,1)S(1)} all-gather(bf16[1,1,128]{2,1,0:T(2,128)(2,1)} %bitcast.499), channel_id=1, replica_groups=mesh['ctx'=8,'heads'=4] {'ctx'}, dimensions={0}, use_global_device_ids=true | all-gather | bytes 2304 | tf_op jit(solution)/shard_map/all_gather | solution.py:67
  35.0 76.9 %all-gather.7.cloned.1.call-done = bf16[1024,3072]{1,0:T(8,128)(2,1)} async-done(((bf16[128,3072]{1,0:T(8,128)(2,1)}), bf16[1024,3072]{1,0:T(8,128)(2,1)}) %all-gather.7.cloned.1.call-update) | async-done | bytes 6291472 | tf_op jit(solution)/shard_map/all_gather | solution.py:63
  123.2 11.0 all-to-all-done.1
  156.9 14.8 %collective-permute-done = s32[512]{0:T(512)S(1)} collective-permute-done((s32[512]{0:T(512)S(1)}, s32[512]{0:T(512)S(1)}, u32[]{:S(2)}, u32[]{:S(2)}) %collective-permute-start) | collective-permute-done | bytes 2080 | tf_op jit(solution)/shard_map/ppermute | solution.py:18
  220.4 11.0 collective-permute-done.11
  232.4 8.4 collective-permute-done.12
  241.7 17.0 %collective-permute-done.13 = bf16[512,2,256]{2,0,1:T(8,128)(2,1)S(1)} collective-permute-done((bf16[512,2,256]{2,0,1:T(8,128)(2,1)}, bf16[512,2,256]{2,0,1:T(8,128)(2,1)S(1)}, u32[]{:S(2)}, u32[]{:S(2)}) %collective-permute-start.13) | collective-permute-done | bytes 524320 | tf_op jit(solution)/shard_map/ppermute | solution.py:18
  262.9 48.3 %collective-permute-done.15 = bf16[512,2,256]{2,0,1:T(8,128)(2,1)S(1)} collective-permute-done((bf16[512,2,256]{2,0,1:T(8,128)(2,1)}, bf16[512,2,256]{2,0,1:T(8,128)(2,1)S(1)}, u32[]{:S(2)}, u32[]{:S(2)}) %collective-permute-start.15) | collective-permute-done | bytes 524320 | tf_op jit(solution)/shard_map/ppermute | solution.py:18
  319.6 41.2 %while.42 = (s32[]{:T(128)}, f32[4,512]{1,0:T(4,128)S(1)}, f32[4,512]{1,0:T(4,128)S(1)}, s32[512]{0:T(512)S(1)}, s32[9,512]{1,0:T(8,128)S(1)}, /*index=5*/bf16[9...) while((s32[]{:T(128)}, f32[4,512]{1,0:T(4,128)S(1)}, ...), condition=%wide.region_7.8_spmd, body=%wide.region_2.7_spmd.sunk | while | flops 142872576 | bytes 11387163 | solution.py:146
  360.9 40.8 %while.43 = (s32[]{:T(128)}, f32[512,4,64]{0,2,1:T(8,128)S(1)}, s32[512]{0:T(512)S(1)}, s32[9,512]{1,0:T(8,128)S(1)}, bf16[9,512,2,256]{1,3,2,0:T(8,128)(2,1)}, ...) while((s32[]{:T(128)}, f32[512,4,64]{0,2,1:T(8,128)S(1)}, ...), condition=%wide.region_11.12_spmd, body=%wide.region_8.11_spmd.sunk | while | flops 274071552 | bytes 4473083 | solution.py:146
  406.1 24.0 %all-gather.1 = bf16[8,1,128]{2,1,0:T(2,128)(2,1)S(1)} all-gather(bf16[1,1,128]{2,1,0:T(2,128)(2,1)S(1)} %bitcast.500), channel_id=1, replica_groups=mesh['ctx'=8,'heads'=4] {'ctx'}, dimensions={0}, use_global_device_ids=true | all-gather | bytes 2304 | tf_op jit(solution)/shard_map/all_gather | solution.py:68
  439.9 30.5 %all-gather.13.cloned.1.call-done = bf16[2624,1024]{1,0:T(8,128)(2,1)} async-done(((bf16[2624,128]{1,0:T(8,128)(2,1)}), bf16[2624,1024]{1,0:T(8,128)(2,1)}) %all-gather.13.cloned.1.call-update) | async-done | bytes 5373968 | tf_op jit(solution)/shard_map/all_gather | solution.py:66
  470.4 8.6 add_convert_fusion
  544.1 14.1 %conditional.11 = (f32[512,4,64]{0,2,1:T(8,128)S(1)}, f32[512,2,256]{2,0,1:T(8,128)}) conditional(s32[]{:T(128)} %bitcast.139, (f32[512,4,64]{0,2,1:T(8,128)S(1)}, f32[512,2,256]{0,2,1:T(8,128)S(1)}) %tuple.188, (s32[512]{0:T(512)S(1)}, bf16[512,2,256]{2,0,1:T(8,128)(2,1)}, bf16[512,4,64]{0,2,1:T(8,128)(2,1)S(1)}, f32[4,512]{1,0:T(4,128)S(1)}, ...), branch_computations={%region_17.18_spmd, %region_18.19_spmd} | conditional | flops 684851200 | bytes 41445476 | solution.py:286
  559.6 10.0 conditional.13
  581.5 16.8 %collective-permute-start.23 = (bf16[512,2,256]{2,0,1:T(8,128)(2,1)}, bf16[512,2,256]{2,0,1:T(8,128)(2,1)}, u32[]{:S(2)}, u32[]{:S(2)}) collective-permute-start(bf16[512,2,256]{2,0,1:T(8,128)(2,1)} %copy.209), channel_id=1, source_target_pairs={{0,16},{4,20},{8,24},{12,28},{1,17},{5,21},{9,25},{13,29},{2,18},{... | collective-permute-start | bytes 1572872 | tf_op jit(solution)/shard_map/ppermute | solution.py:18
  627.8 25.7 %collective-permute-done.22 = bf16[512,2,256]{2,0,1:T(8,128)(2,1)} collective-permute-done((bf16[512,2,256]{2,0,1:T(8,128)(2,1)}, bf16[512,2,256]{2,0,1:T(8,128)(2,1)}, u32[]{:S(2)}, u32[]{:S(2)}) %collective-permute-start.22) | collective-permute-done | bytes 524320 | tf_op jit(solution)/shard_map/ppermute | solution.py:18
  656.2 13.0 %collective-permute-done.18 = bf16[512,2,256]{2,0,1:T(8,128)(2,1)S(1)} collective-permute-done((bf16[512,2,256]{2,0,1:T(8,128)(2,1)}, bf16[512,2,256]{2,0,1:T(8,128)(2,1)S(1)}, u32[]{:S(2)}, u32[]{:S(2)}) %collective-permute-start.18) | collective-permute-done | bytes 524320 | tf_op jit(solution)/shard_map/ppermute | solution.py:18
  669.2 21.4 %collective-permute-done.17 = bf16[512,2,256]{2,0,1:T(8,128)(2,1)S(1)} collective-permute-done((bf16[512,2,256]{2,0,1:T(8,128)(2,1)}, bf16[512,2,256]{2,0,1:T(8,128)(2,1)S(1)}, u32[]{:S(2)}, u32[]{:S(2)}) %collective-permute-start.17) | collective-permute-done | bytes 524320 | tf_op jit(solution)/shard_map/ppermute | solution.py:18
  693.7 17.3 %all_to_all.75 = bf16[512,3,1,256]{3,1,2,0:T(4,128)(2,1)S(1)} all-to-all(bf16[512,3,1,256]{3,1,2,0:T(4,128)(2,1)S(1)} %copy.211), channel_id=1, replica_groups=mesh['ctx'=8,'heads'=4] {'heads'}, dimensions={0} | all-to-all | bytes 1572864 | tf_op jit(solution)/shard_map/all_to_all | solution.py:301
  732.0 106.0 %reduce-scatter.7.cloned.1.call-done = bf16[128,3072]{1,0:T(8,128)(2,1)} async-done(((bf16[1024,3072]{1,0:T(8,128)(2,1)}), bf16[128,3072]{1,0:T(8,128)(2,1)}) %reduce-scatter.7.cloned.1.call-update) | async-done | bytes 786448 | tf_op jit(solution)/shard_map/reduce_scatter | solution.py:321
  838.0 184.9 %reduce-scatter.11.cloned.1.call-done = bf16[128,5248]{1,0:T(8,128)(2,1)} async-done(((bf16[1024,5248]{1,0:T(8,128)(2,1)}), bf16[128,5248]{1,0:T(8,128)(2,1)}) %reduce-scatter.11.cloned.1.call-update) | async-done | bytes 1343504 | tf_op jit(solution)/shard_map/reduce_scatter | solution.py:327
  1032.3 19.5 %all-reduce.2 = (bf16[1024]{0:T(1024)(128)(2,1)S(1)}, bf16[1024]{0:T(1024)(128)(2,1)S(1)}) all-reduce(bf16[1024]{0:T(1024)(128)(2,1)S(1)} %get-tuple-element.1818, bf16[1024]{0:T(1024)(128)(2,1)S(1)} %get-tuple-element.1816), channel_id=6, replica_groups=mesh['ctx'=8,'heads'=4] {'ctx'}, use_global_device_ids=true, to_apply=%region_46.47.clone | all-reduce | flops 2048 | bytes 8192
  1060.3 33.0 %all-reduce.7.cloned.1.call-done = (bf16[128,3072]{1,0:T(8,128)(2,1)}, bf16[128,1024]{1,0:T(8,128)(2,1)}, bf16[128,5248]{1,0:T(8,128)(2,1)}, bf16[2624,128]{1,0:T(8,128)(2,1)}) async-done(((bf16[128,3072]{1,0:T(8,128)(2,1)}, bf16[128,1024]{1,0:T(8,128)(2,1)}, bf16[128,5248]{1,0:T(8,128)(2,1)}, bf16[2624,128]{1,0:T(8,128)(2,1)}), (bf16[128,3072]{1,0:T(8,128)(2,1)}, bf16[128,1024]{1,0:T(8,128)(2,1)}, ...) | async-done | bytes 3063824 | tf_op jit(solution)/shard_map/psum | solution.py:341
  (389 shorter events, 329.4 us)
Async XLA Ops:
  7.2 104.8 %all-gather.7.cloned.1.call-start = ((), (), s32[]{:S(2)}) async-start(), calls=%async_computation.9 | async-start | bytes 7077888 | tf_op jit(solution)/shard_map/all_gather | solution.py:63
  7.9 422.2 %all-gather.9.cloned.1.call-start = ((), (), s32[]{:S(2)}) async-start(), calls=%async_computation.10 | async-start | bytes 2359296 | tf_op jit(solution)/shard_map/all_gather | solution.py:64
  8.7 423.9 %all-gather.11.cloned.1.call-start = ((), (), s32[]{:S(2)}) async-start(), calls=%async_computation.11 | async-start | bytes 12091392 | tf_op jit(solution)/shard_map/all_gather | solution.py:65
  122.6 347.8 %all-gather.13.cloned.1.call-start = ((), (), s32[]{:S(2)}) async-start(), calls=%async_computation.12 | async-start | bytes 6045696 | tf_op jit(solution)/shard_map/all_gather | solution.py:66
  135.3 68.4 %collective-permute-start.8 = (bf16[512,2,256]{2,0,1:T(8,128)(2,1)}, bf16[512,2,256]{2,0,1:T(8,128)(2,1)S(1)}, u32[]{:S(2)}, u32[]{:S(2)}) collective-permute-start(bf16[512,2,256]{2,0,1:T(8,128)(2,1)} %slice_bitcast_fusion.2), channel_id=1, source_target_pairs={{0,4},{4,8},{8,12},{12,16},{16,20},{20,24},{24,28},{1,5},{5,9},{9,... | collective-permute-start | bytes 1572872 | tf_op jit(solution)/shard_map/ppermute | solution.py:18
  137.8 68.0 %collective-permute-start.9 = (bf16[512,2,256]{2,0,1:T(8,128)(2,1)}, bf16[512,2,256]{2,0,1:T(8,128)(2,1)S(1)}, u32[]{:S(2)}, u32[]{:S(2)}) collective-permute-start(bf16[512,2,256]{2,0,1:T(8,128)(2,1)} %slice_bitcast_fusion.2), channel_id=1, source_target_pairs={{4,0},{8,4},{12,8},{16,12},{20,16},{24,20},{28,24},{5,1},{9,5},{13... | collective-permute-start | bytes 1572872 | tf_op jit(solution)/shard_map/ppermute | solution.py:18
  195.4 36.1 %collective-permute-start.11 = (bf16[512,2,256]{2,0,1:T(8,128)(2,1)}, bf16[512,2,256]{2,0,1:T(8,128)(2,1)S(1)}, u32[]{:S(2)}, u32[]{:S(2)}) collective-permute-start(bf16[512,2,256]{2,0,1:T(8,128)(2,1)} %slice_bitcast_fusion.2), channel_id=1, source_target_pairs={{8,0},{12,4},{16,8},{20,12},{24,16},{28,20},{9,1},{13,5},{17,9},{2... | collective-permute-start | bytes 1572872 | tf_op jit(solution)/shard_map/ppermute | solution.py:18
  196.7 44.1 %collective-permute-start.12 = (bf16[512,2,256]{2,0,1:T(8,128)(2,1)}, bf16[512,2,256]{2,0,1:T(8,128)(2,1)S(1)}, u32[]{:S(2)}, u32[]{:S(2)}) collective-permute-start(bf16[512,2,256]{2,0,1:T(8,128)(2,1)} %slice_bitcast_fusion.2), channel_id=1, source_target_pairs={{0,12},{4,16},{8,20},{12,24},{16,28},{1,13},{5,17},{9,21},{13,25},... | collective-permute-start | bytes 1572872 | tf_op jit(solution)/shard_map/ppermute | solution.py:18
  203.7 55.0 %collective-permute-start.13 = (bf16[512,2,256]{2,0,1:T(8,128)(2,1)}, bf16[512,2,256]{2,0,1:T(8,128)(2,1)S(1)}, u32[]{:S(2)}, u32[]{:S(2)}) collective-permute-start(bf16[512,2,256]{2,0,1:T(8,128)(2,1)} %slice_bitcast_fusion.2), channel_id=1, source_target_pairs={{12,0},{16,4},{20,8},{24,12},{28,16},{13,1},{17,5},{21,9},{25,13},... | collective-permute-start | bytes 1572872 | tf_op jit(solution)/shard_map/ppermute | solution.py:18
  205.8 56.3 %collective-permute-start.14 = (bf16[512,2,256]{2,0,1:T(8,128)(2,1)}, bf16[512,2,256]{2,0,1:T(8,128)(2,1)S(1)}, u32[]{:S(2)}, u32[]{:S(2)}) collective-permute-start(bf16[512,2,256]{2,0,1:T(8,128)(2,1)} %slice_bitcast_fusion.2), channel_id=1, source_target_pairs={{0,16},{4,20},{8,24},{12,28},{1,17},{5,21},{9,25},{13,29},{2,18},{... | collective-permute-start | bytes 1572872 | tf_op jit(solution)/shard_map/ppermute | solution.py:18
  218.3 92.9 %collective-permute-start.15 = (bf16[512,2,256]{2,0,1:T(8,128)(2,1)}, bf16[512,2,256]{2,0,1:T(8,128)(2,1)S(1)}, u32[]{:S(2)}, u32[]{:S(2)}) collective-permute-start(bf16[512,2,256]{2,0,1:T(8,128)(2,1)} %slice_bitcast_fusion.2), channel_id=1, source_target_pairs={{16,0},{20,4},{24,8},{28,12},{17,1},{21,5},{25,9},{29,13},{18,2},{... | collective-permute-start | bytes 1572872 | tf_op jit(solution)/shard_map/ppermute | solution.py:18
  406.0 323.8 %reduce-scatter.13.cloned.1.call-start = ((), (), s32[]{:S(2)}) async-start(), calls=%async_computation.16 | async-start | bytes 6193152
  492.4 239.6 %reduce-scatter.9.cloned.1.call-start = ((), (), s32[]{:S(2)}) async-start(), calls=%async_computation.14 | async-start | bytes 2359296 | tf_op jit(solution)/shard_map/reduce_scatter | solution.py:324
  532.7 305.3 %reduce-scatter.7.cloned.1.call-start = ((), (), s32[]{:S(2)}) async-start(), calls=%async_computation.13 | async-start | bytes 7077888 | tf_op jit(solution)/shard_map/reduce_scatter | solution.py:321
  581.5 45.0 %collective-permute-start.23 = (bf16[512,2,256]{2,0,1:T(8,128)(2,1)}, bf16[512,2,256]{2,0,1:T(8,128)(2,1)}, u32[]{:S(2)}, u32[]{:S(2)}) collective-permute-start(bf16[512,2,256]{2,0,1:T(8,128)(2,1)} %copy.209), channel_id=1, source_target_pairs={{0,16},{4,20},{8,24},{12,28},{1,17},{5,21},{9,25},{13,29},{2,18},{... | collective-permute-start | bytes 1572872 | tf_op jit(solution)/shard_map/ppermute | solution.py:18
  600.6 53.0 %collective-permute-start.22 = (bf16[512,2,256]{2,0,1:T(8,128)(2,1)}, bf16[512,2,256]{2,0,1:T(8,128)(2,1)}, u32[]{:S(2)}, u32[]{:S(2)}) collective-permute-start(bf16[512,2,256]{2,0,1:T(8,128)(2,1)} %copy.208), channel_id=1, source_target_pairs={{16,0},{20,4},{24,8},{28,12},{17,1},{21,5},{25,9},{29,13},{18,2},{... | collective-permute-start | bytes 1572872 | tf_op jit(solution)/shard_map/ppermute | solution.py:18
  604.1 50.8 %collective-permute-start.21 = (bf16[512,2,256]{2,0,1:T(8,128)(2,1)}, bf16[512,2,256]{2,0,1:T(8,128)(2,1)}, u32[]{:S(2)}, u32[]{:S(2)}) collective-permute-start(bf16[512,2,256]{2,0,1:T(8,128)(2,1)} %copy.207), channel_id=1, source_target_pairs={{0,12},{4,16},{8,20},{12,24},{16,28},{1,13},{5,17},{9,21},{13,25},... | collective-permute-start | bytes 1572872 | tf_op jit(solution)/shard_map/ppermute | solution.py:18
  609.8 46.4 %collective-permute-start.20 = (bf16[512,2,256]{2,0,1:T(8,128)(2,1)}, bf16[512,2,256]{2,0,1:T(8,128)(2,1)}, u32[]{:S(2)}, u32[]{:S(2)}) collective-permute-start(bf16[512,2,256]{2,0,1:T(8,128)(2,1)} %copy.206), channel_id=1, source_target_pairs={{12,0},{16,4},{20,8},{24,12},{28,16},{13,1},{17,5},{21,9},{25,13},... | collective-permute-start | bytes 1572872 | tf_op jit(solution)/shard_map/ppermute | solution.py:18
  613.3 42.9 %collective-permute-start.19 = (bf16[512,2,256]{2,0,1:T(8,128)(2,1)}, bf16[512,2,256]{2,0,1:T(8,128)(2,1)}, u32[]{:S(2)}, u32[]{:S(2)}) collective-permute-start(bf16[512,2,256]{2,0,1:T(8,128)(2,1)} %copy.205), channel_id=1, source_target_pairs={{0,8},{4,12},{8,16},{12,20},{16,24},{20,28},{1,9},{5,13},{9,17},{1... | collective-permute-start | bytes 1572872 | tf_op jit(solution)/shard_map/ppermute | solution.py:18
  626.5 42.7 %collective-permute-start.18 = (bf16[512,2,256]{2,0,1:T(8,128)(2,1)}, bf16[512,2,256]{2,0,1:T(8,128)(2,1)S(1)}, u32[]{:S(2)}, u32[]{:S(2)}) collective-permute-start(bf16[512,2,256]{2,0,1:T(8,128)(2,1)} %copy.204), channel_id=1, source_target_pairs={{8,0},{12,4},{16,8},{20,12},{24,16},{28,20},{9,1},{13,5},{17,9},{2... | collective-permute-start | bytes 1572872 | tf_op jit(solution)/shard_map/ppermute | solution.py:18
  653.6 37.0 %collective-permute-start.17 = (bf16[512,2,256]{2,0,1:T(8,128)(2,1)}, bf16[512,2,256]{2,0,1:T(8,128)(2,1)S(1)}, u32[]{:S(2)}, u32[]{:S(2)}) collective-permute-start(bf16[512,2,256]{2,0,1:T(8,128)(2,1)} %copy.203), channel_id=1, source_target_pairs={{0,4},{4,8},{8,12},{12,16},{16,20},{20,24},{24,28},{1,5},{5,9},{9,... | collective-permute-start | bytes 1572872 | tf_op jit(solution)/shard_map/ppermute | solution.py:18
  654.9 35.7 %collective-permute-start.16 = (bf16[512,2,256]{2,0,1:T(8,128)(2,1)S(1)}, bf16[512,2,256]{2,0,1:T(8,128)(2,1)S(1)}, u32[]{:S(2)}, u32[]{:S(2)}) collective-permute-start(bf16[512,2,256]{2,0,1:T(8,128)(2,1)S(1)} %copy.201), channel_id=1, source_target_pairs={{4,0},{8,4},{12,8},{16,12},{20,16},{24,20},{28,24},{5,1},{9,5},{13... | collective-permute-start | bytes 1572872 | tf_op jit(solution)/shard_map/ppermute | solution.py:18
  719.9 303.1 %reduce-scatter.11.cloned.1.call-start = ((), (), s32[]{:S(2)}) async-start(), calls=%async_computation.15 | async-start | bytes 12091392 | tf_op jit(solution)/shard_map/reduce_scatter | solution.py:327
  727.9 365.3 %all-reduce.7.cloned.1.call-start = ((), (), s32[]{:S(2)}) async-start(), calls=%async_computation.17 | async-start | bytes 6127616 | tf_op jit(solution)/shard_map/psum | solution.py:341
  (54 other events, 1744.2 us)
Sparse Core Ops, SparseCore 0:
  10.2 101.7 all-gather.6
  114.1 69.0 all-gather.8
  185.3 196.9 all-gather.10
  384.3 86.0 all-gather.12
  492.5 104.4 reduce-scatter.12
  601.4 115.4 reduce-scatter.8
  720.9 117.0 reduce-scatter.6
  842.1 180.8 reduce-scatter.10
  1026.2 67.0 all-reduce.6
where the time goes:
time: 1120 us; the launch traced here: 1110 us
  waiting for transfers between devices  619 us (55%)
  local copies, waits for them, and re-layouts  103 us (9%)
  blocking collectives  95.6 us (9%)
  starting transfers between devices  92.6 us (8%)
  matrix products  79 us (7%)
  loops' own time  54.1 us (5%)
  between operations  38.1 us (3%)
  other arithmetic  25.2 us (2%)
    reduce_scatter x1, waiting for transfers between devices, body(): lax.psum_scatter(grad_w_in.astype(jnp.bfloat16), 'ctx', scatter_dimension...  185 us
    ppermute x24, waiting for transfers between devices, passed_along(): lax.ppermute(value, axis, [(source, source + steps) for source in range(i...  174 us
    reduce_scatter x1, waiting for transfers between devices, body(): lax.psum_scatter(grad_w_qkv.astype(jnp.bfloat16), 'ctx', scatter_dimensio...  106 us
    ppermute x24, starting transfers between devices, passed_along(): lax.ppermute(value, axis, [(source, source + steps) for source in range(i...  81.1 us
    all_gather x1, waiting for transfers between devices, body(): lax.all_gather(w_qkv, 'ctx', axis=0, tiled=True)  76.9 us
    another operation x2, loops' own time, sweep(): return lax.fori_loop(0, block_count * tile_count, sweep_visit, initial)  47.4 us
    psum x1, waiting for transfers between devices, body(): lax.psum(reduced[0].astype(jnp.bfloat16), 'heads').astype(jnp.float32)  33 us
    all_gather x1, waiting for transfers between devices, body(): lax.all_gather(w_out, 'ctx', axis=1, tiled=True)  30.5 us
  transfers between devices with their start and end apart: 36, of which 17 were waited for; matrix products, arithmetic and copies ran while one was open for 16% of the time, Pallas kernels for 0%

commit v1 on v0

v1 whole, which is shorter than its diff:
```python
import functools

import jax
import jax.numpy as jnp
from jax import lax
from jax.experimental import pallas as pl
from jax.experimental.pallas import tpu as pltpu
from jax.sharding import PartitionSpec as P

H = 16
HD = 64
HALF = HD // 2
FF = 2624
SEQ_MAX = 2048
MASKED = -1e30
MARKS = 16
Q_END = HD
QM_END = Q_END + MARKS
K_END = QM_END + HD
KM_END = K_END + MARKS
V_END = KM_END + HD
BF = jnp.bfloat16
F32 = jnp.float32


def dot(left, right, left_dim, right_dim):
    return lax.dot_general(
        left, right, (((left_dim,), (right_dim,)), ((), ())), preferred_element_type=F32
    )


def norm_parts(values):
    average = jnp.mean(values, axis=-1, keepdims=True)
    centred = values - average
    inverse_std = lax.rsqrt(jnp.mean(centred * centred, axis=-1, keepdims=True) + 1e-05)
    return centred * inverse_std, inverse_std


def norm_back(upstream, normed, inverse_std, gain):
    scaled = upstream * gain
    return inverse_std * (
        scaled
        - jnp.mean(scaled, axis=-1, keepdims=True)
        - normed * jnp.mean(scaled * normed, axis=-1, keepdims=True)
    )


def attend_kernel(tile, qkv_ref, out_ref, wide_ref, lse_ref):
    blocks, _, block = qkv_ref.shape
    per_block = block // tile
    step = pl.program_id(0)
    which = step // per_block
    start = pl.multiple_of(step % per_block * tile, tile)
    query = qkv_ref[which, :QM_END, pl.ds(start, tile)]
    scores = [dot(qkv_ref[j, QM_END:KM_END, :], query, 0, 0) for j in range(blocks)]
    top = functools.reduce(jnp.maximum, [jnp.max(s, axis=0, keepdims=True) for s in scores])
    raised = [jnp.exp(s - top) for s in scores]
    total = functools.reduce(jnp.add, [jnp.sum(e, axis=0, keepdims=True) for e in raised])
    scale = 1.0 / total
    result = jnp.zeros((HD, tile), F32)
    for j in range(blocks):
        result += dot(qkv_ref[j, KM_END:V_END, :], (raised[j] * scale).astype(BF), 1, 0)
    out_ref[which, :, pl.ds(start, tile)] = result.astype(BF)
    wide_ref[which, :, pl.ds(start, tile)] = result
    lse_ref[which, :, pl.ds(start, tile)] = top + jnp.log(total)


def attend(qkv, tile):
    blocks, _, block = qkv.shape
    whole = lambda rows: pl.BlockSpec((blocks, rows, block), lambda i: (0, 0, 0))
    count = blocks * block
    return pl.pallas_call(
        functools.partial(attend_kernel, tile),
        grid=(count // tile,),
        in_specs=[whole(V_END)],
        out_specs=[whole(HD), whole(HD), whole(1)],
        out_shape=[
            jax.ShapeDtypeStruct((blocks, HD, block), BF),
            jax.ShapeDtypeStruct((blocks, HD, block), F32),
            jax.ShapeDtypeStruct((blocks, 1, block), F32),
        ],
        compiler_params=pltpu.CompilerParams(vmem_limit_bytes=40 << 20),
        cost_estimate=pl.CostEstimate(
            flops=count * count * HD * 8, bytes_accessed=count * 1024, transcendentals=count * count
        ),
        name="attend",
    )(qkv)


def attend_back_kernel(tile, qkv_ref, grad_ref, wide_ref, lse_ref, out_ref, sums):
    blocks, _, block = qkv_ref.shape
    per_block = block // tile
    step = pl.program_id(0)

    @pl.when(step == 0)
    def _():
        sums[...] = jnp.zeros_like(sums)

    which = step // per_block
    start = pl.multiple_of(step % per_block * tile, tile)
    query = qkv_ref[which, :QM_END, pl.ds(start, tile)]
    grad = grad_ref[which, :, pl.ds(start, tile)]
    delta = jnp.sum(
        grad.astype(F32) * wide_ref[which, :, pl.ds(start, tile)], axis=0, keepdims=True
    )
    lse = lse_ref[which, :, pl.ds(start, tile)]
    grad_query = jnp.zeros((HD, tile), F32)
    for j in range(blocks):
        prob = jnp.exp(dot(qkv_ref[j, QM_END:KM_END, :], query, 0, 0) - lse)
        grad_prob = dot(qkv_ref[j, KM_END:V_END, :], grad, 0, 0)
        grad_score = (prob * (grad_prob - delta)).astype(BF)
        grad_query += dot(qkv_ref[j, QM_END:K_END, :], grad_score, 1, 0)
        sums[j, :HD, :] += dot(query[:HD], grad_score, 1, 1)
        sums[j, HD:, :] += dot(grad, prob.astype(BF), 1, 1)
    out_ref[which, :HD, pl.ds(start, tile)] = (grad_query * 0.125).astype(BF)

    @pl.when(step == pl.num_programs(0) - 1)
    def _():
        out_ref[:, HD:, :] = sums[...].astype(BF)


def attend_back(qkv, grad, wide, lse, tile):
    blocks, _, block = qkv.shape
    whole = lambda rows: pl.BlockSpec((blocks, rows, block), lambda i: (0, 0, 0))
    count = blocks * block
    return pl.pallas_call(
        functools.partial(attend_back_kernel, tile),
        grid=(count // tile,),
        in_specs=[whole(V_END), whole(HD), whole(HD), whole(1)],
        out_specs=whole(3 * HD),
        out_shape=jax.ShapeDtypeStruct((blocks, 3 * HD, block), BF),
        scratch_shapes=[pltpu.VMEM((blocks, 2 * HD, block), F32)],
        compiler_params=pltpu.CompilerParams(vmem_limit_bytes=40 << 20),
        cost_estimate=pl.CostEstimate(
            flops=count * count * HD * 20, bytes_accessed=count * 1536, transcendentals=count * count
        ),
        name="attend_back",
    )(qkv, grad, wide, lse)


def body(tokens, d_out, segment_ids, position_ids, w_qkv, w_attn, w_in, w_out, gain_attn, gain_mlp):
    groups = lax.axis_size("heads")
    ctx_count = lax.axis_size("ctx")
    member = lax.axis_index("heads")
    rows, width = tokens.shape
    shard = w_qkv.shape[0]
    block = rows * groups
    reach = SEQ_MAX // block
    per_group = H // groups
    assert per_group == reach
    lanes = per_group * HD
    hidden = FF // groups
    padded = -(-hidden // 128) * 128
    tile = min(512, block)
    teams = [[reach * i + j for j in range(reach)] for i in range(ctx_count // reach)]

    def swap(value):
        return lax.all_to_all(
            value, "ctx", split_axis=0, concat_axis=0, axis_index_groups=teams, tiled=True
        )

    def own_rows(value):
        return lax.dynamic_slice_in_dim(value, member * rows, rows, 0)

    def heads_sum(value):
        parts = lax.all_to_all(
            value.astype(BF).reshape(groups, rows, width),
            "heads",
            split_axis=0,
            concat_axis=0,
            tiled=True,
        )
        return jnp.sum(parts.astype(F32), axis=0)

    extra = jnp.stack([position_ids // 256, position_ids % 256, segment_ids % 2], axis=1)
    extra = jnp.pad(extra.astype(BF), ((0, 0), (0, 125)))
    gathered_block = lax.all_gather(
        jnp.concatenate([tokens, d_out, extra], axis=1), "heads", axis=0, tiled=True
    )
    qkv_part = lax.dynamic_slice_in_dim(
        w_qkv.reshape(shard, 3, width), member * lanes, lanes, 2
    ).reshape(shard, 3 * lanes)
    gains = jnp.pad(jnp.stack([gain_attn, gain_mlp], axis=1), ((0, 0), (0, 126)))
    first_weights = lax.all_gather(
        jnp.concatenate([qkv_part, gains], axis=1), "ctx", axis=0, tiled=True
    )

    def fit(value):
        return jnp.pad(value, ((0, 0), (0, padded - hidden)))

    left_part = fit(lax.dynamic_slice_in_dim(w_in, member * hidden, hidden, 1))
    right_part = fit(lax.dynamic_slice_in_dim(w_in, FF + member * hidden, hidden, 1))
    out_part = fit(lax.dynamic_slice_in_dim(w_out, member * hidden, hidden, 0).T)
    full_attn = lax.all_gather(w_attn, "ctx", axis=0, tiled=True)
    mlp_weights = lax.all_gather(
        jnp.concatenate([left_part, right_part, out_part], axis=1), "ctx", axis=0, tiled=True
    )
    in_weights = mlp_weights[:, : 2 * padded]
    out_weights = mlp_weights[:, 2 * padded :]

    residual_in = gathered_block[:, :width].astype(F32)
    upstream = gathered_block[:, width : 2 * width]
    digits = gathered_block[:, 2 * width :].astype(F32)
    positions = digits[:, 0] * 256.0 + digits[:, 1]
    parity = digits[:, 2][None, :]
    freqs = jnp.power(160000.0, -(2.0 * jnp.arange(HALF, dtype=F32)) / HD)
    angles = freqs[:, None] * positions[None, :]
    cosine = jnp.cos(angles)
    sine = jnp.sin(angles)

    qkv_weights = first_weights[:, : 3 * lanes]
    gain_one = first_weights[:, 3 * lanes].astype(F32)
    gain_two = first_weights[:, 3 * lanes + 1].astype(F32)
    plain_one, inverse_one = norm_parts(residual_in)
    attn_input = (plain_one * gain_one).astype(BF)
    projected = dot(qkv_weights, attn_input, 0, 1).reshape(3, per_group, 2, HALF, block)

    def turn(value):
        front, back = value[:, 0], value[:, 1]
        return jnp.concatenate([front * cosine - back * sine, back * cosine + front * sine], axis=1)

    def mark_rows(first, second):
        pad = jnp.zeros((MARKS - 2, block), F32)
        stacked = jnp.concatenate([first, second, pad], axis=0)
        return jnp.broadcast_to(stacked[None], (per_group, MARKS, block))

    outgoing = jnp.concatenate(
        [
            turn(projected[0]) * 0.125,
            mark_rows(parity, 1.0 - parity),
            turn(projected[1]),
            mark_rows((1.0 - parity) * MASKED, parity * MASKED),
            projected[2].reshape(per_group, HD, block),
        ],
        axis=1,
    ).astype(BF)
    qkv = swap(outgoing)
    attended, attended_wide, lse = attend(qkv, tile)
    returned = swap(attended).reshape(lanes, block)
    attended_all = lax.all_gather(returned, "heads", axis=0, tiled=True)
    middle = residual_in + dot(attended_all, full_attn, 0, 0)
    plain_two, inverse_two = norm_parts(middle)
    mlp_input = (plain_two * gain_two).astype(BF)
    gate_up = dot(mlp_input, in_weights, 1, 0)
    gate_left = gate_up[:, :padded]
    gate_right = gate_up[:, padded:]
    normal_cdf = 0.5 * (1.0 + lax.erf(gate_left * 0.7071067811865476))
    gelu = gate_left * normal_cdf
    density = jnp.exp(-0.5 * gate_left * gate_left) * 0.3989422804014327
    mixed = (gelu * gate_right).astype(BF)
    grad_mixed = dot(upstream, out_weights, 1, 0)
    grad_left = grad_mixed * gate_right * (normal_cdf + gate_left * density)
    grad_gate_up = jnp.concatenate([grad_left, grad_mixed * gelu], axis=1).astype(BF)
    grad_mlp_part = dot(grad_gate_up, in_weights, 1, 1)
    grad_gain_two = jnp.sum(grad_mlp_part * plain_two, axis=0)
    grad_norm_mid = norm_back(
        heads_sum(grad_mlp_part), own_rows(plain_two), own_rows(inverse_two), gain_two
    )
    grad_middle = d_out.astype(F32) + grad_norm_mid
    grad_branch = lax.all_gather(grad_middle.astype(BF), "heads", axis=0, tiled=True)
    attn_rows = lax.dynamic_slice_in_dim(full_attn, member * lanes, lanes, 0)
    grad_attended = dot(attn_rows, grad_branch, 1, 1).astype(BF).reshape(per_group, HD, block)
    grad_heads = swap(grad_attended)
    result = (own_rows(middle) + heads_sum(dot(mixed, out_weights, 1, 1))).astype(BF)
    grad_out_part = dot(upstream, mixed, 0, 0)
    grad_in_part = dot(mlp_input, grad_gate_up, 0, 0)
    branch_columns = lax.dynamic_slice_in_dim(grad_branch, member * lanes, lanes, 1)
    grad_attn_part = dot(attended_all, branch_columns, 1, 0)
    late = lax.psum_scatter(
        jnp.concatenate([grad_in_part, grad_out_part, grad_attn_part], axis=1).astype(BF),
        "ctx",
        scatter_dimension=0,
        tiled=True,
    )
    grad_qkv = swap(attend_back(qkv, grad_heads, attended_wide, lse, tile))
    grad_qkv = grad_qkv.astype(F32).reshape(per_group, 3, 2, HALF, block)

    def turn_back(value):
        front, back = value[:, 0], value[:, 1]
        return jnp.stack([front * cosine + back * sine, back * cosine - front * sine], axis=1)

    grad_projected = (
        jnp.stack([turn_back(grad_qkv[:, 0]), turn_back(grad_qkv[:, 1]), grad_qkv[:, 2]])
        .reshape(3 * lanes, block)
        .astype(BF)
    )
    grad_attn_in = dot(grad_projected, qkv_weights, 0, 1)
    grad_gain_one = jnp.sum(grad_attn_in * plain_one, axis=0)
    grad_qkv_part = dot(attn_input, grad_projected, 0, 1)
    grad_gains = jnp.pad(jnp.stack([grad_gain_one, grad_gain_two], axis=1), ((0, 0), (0, 126)))
    last = lax.psum_scatter(
        jnp.concatenate([grad_qkv_part, grad_gains], axis=1).astype(BF),
        "ctx",
        scatter_dimension=0,
        tiled=True,
    )
    grad_input = grad_middle + norm_back(
        heads_sum(grad_attn_in), own_rows(plain_one), own_rows(inverse_one), gain_one
    )
    late_all = lax.all_gather(late, "heads", axis=0)
    last_all = lax.all_gather(last, "heads", axis=0)
    sum_qkv = (
        last_all[:, :, : 3 * lanes]
        .reshape(groups, shard, 3, lanes)
        .transpose(1, 2, 0, 3)
        .reshape(shard, 3 * width)
        .astype(F32)
    )
    gain_sums = jnp.sum(last_all[:, :, 3 * lanes : 3 * lanes + 2].astype(F32), axis=0)

    def columns(start, size):
        piece = late_all[:, :, start : start + size]
        return piece.transpose(1, 0, 2).reshape(shard, groups * size).astype(F32)

    sum_in = jnp.concatenate([columns(0, hidden), columns(padded, hidden)], axis=1)
    sum_out = (
        late_all[:, :, 2 * padded : 2 * padded + hidden]
        .transpose(0, 2, 1)
        .reshape(groups * hidden, shard)
        .astype(F32)
    )
    sum_attn = columns(3 * padded, lanes)
    return (
        result,
        grad_input,
        sum_qkv,
        sum_attn,
        sum_in,
        sum_out,
        gain_sums[:, 0],
        gain_sums[:, 1],
    )


def solution(mesh):
    return jax.shard_map(
        body,
        mesh=mesh,
        in_specs=(
            P(("ctx", "heads"), None),
            P(("ctx", "heads"), None),
            P(("ctx", "heads")),
            P(("ctx", "heads")),
            P("ctx", None),
            P("ctx", None),
            P("ctx", None),
            P(None, "ctx"),
            P("ctx"),
            P("ctx"),
        ),
        out_specs=(
            P(("ctx", "heads"), None),
            P(("ctx", "heads"), None),
            P("ctx", None),
            P("ctx", None),
            P("ctx", None),
            P(None, "ctx"),
            P("ctx"),
            P("ctx"),
        ),
        check_vma=False,
    )
```

time: 1120 us -> 531 us (0.47); the launches traced: 1110 us -> 529 us
  waiting for transfers between devices: 619 us -> 314 us
  starting transfers between devices: 92.6 us -> 11.1 us
  local copies, waits for them, and re-layouts: 103 us -> 25.1 us
  loops' own time: 54.1 us -> 0 us
  matrix products: 79 us -> 33.8 us
  between operations: 38.1 us -> 14.4 us
  Pallas kernels: 0 us -> 21.4 us
  blocking collectives: 95.6 us -> 78.3 us
    reduce_scatter x3 -> x1, waiting for transfers between devices: 291 us -> 42.3 us  [body(): lax.psum_scatter(jnp.concatenate([grad_in_part, grad_out_part, grad_attn_...]
    ppermute x24 -> x0, waiting for transfers between devices: 174 us -> none  [passed_along(): lax.ppermute(value, axis, [(source, source + steps) for source in range(i...]
    all_gather x4 -> x7, waiting for transfers between devices: 107 us -> 190 us  [the longest x1 77.1 us: body(): lax.all_gather(jnp.concatenate([left_part, right_part, out_part], axis=1)...]
    ppermute x24 -> x0, starting transfers between devices: 81.1 us -> none  [passed_along(): lax.ppermute(value, axis, [(source, source + steps) for source in range(i...]
    another operation x29 -> x0, loops' own time: 54.1 us -> none  [the longest x2 47.4 us: sweep(): return lax.fori_loop(0, block_count * tile_count, sweep_visit, initial)]
    all_to_all x2 -> x4, blocking collectives: 23.4 us -> 68.7 us  [the longest x3 51.7 us: swap(): lax.all_to_all(value, 'ctx', split_axis=0, concat_axis=0, axis_index_grou...]
    dot_general x26 -> x12, matrix products: 79 us -> 33.8 us  [dot(): lax.dot_general(left, right, (((left_dim,), (right_dim,)), ((), ())), pre...]
    all_to_all x3, waiting for transfers between devices: 11 us -> 52.5 us  [the longest x2 26.4 us: heads_sum(): lax.all_to_all(value.astype(BF).reshape(groups, rows, width), 'heads', sp...]
  transfers between devices with their start and end apart: 36 -> 12, of which waited for: 17 -> 12; matrix products, arithmetic and copies ran while one was open for 16% -> 9% of each run, Pallas kernels for 0% -> 4%
where the time goes in v1:
time: 531 us; the launch traced here: 529 us
  waiting for transfers between devices  314 us (59%)
  blocking collectives  78.3 us (15%)
  matrix products  33.8 us (6%)
  other arithmetic  30.8 us (6%)
  local copies, waits for them, and re-layouts  25.1 us (5%)
  Pallas kernels  21.4 us (4%)
  between operations  14.4 us (3%)
  starting transfers between devices  11.1 us (2%)
    all_gather x1, waiting for transfers between devices, body(): lax.all_gather(jnp.concatenate([left_part, right_part, out_part], axis=1)...  77.1 us
    all_to_all x3, blocking collectives, swap(): lax.all_to_all(value, 'ctx', split_axis=0, concat_axis=0, axis_index_grou...  51.7 us
    all_gather x1, waiting for transfers between devices, body(): lax.all_gather(jnp.concatenate([qkv_part, gains], axis=1), 'ctx', axis=0,...  49 us
    reduce_scatter x1, waiting for transfers between devices, body(): lax.psum_scatter(jnp.concatenate([grad_in_part, grad_out_part, grad_attn_...  42.3 us
    dot_general x12, matrix products, dot(): lax.dot_general(left, right, (((left_dim,), (right_dim,)), ((), ())), pre...  33.8 us
    unnamed x10, waiting for transfers between devices  29.8 us
    all_to_all x2, waiting for transfers between devices, heads_sum(): lax.all_to_all(value.astype(BF).reshape(groups, rows, width), 'heads', sp...  26.4 us
    all_to_all x1, waiting for transfers between devices, swap(): lax.all_to_all(value, 'ctx', split_axis=0, concat_axis=0, axis_index_grou...  26.1 us
  transfers between devices with their start and end apart: 12, of which 12 were waited for; matrix products, arithmetic and copies ran while one was open for 9% of the time, Pallas kernels for 4%

profile of v1, /device:TPU:0, one launch (start us, length us, event | category | flops | bytes accessed | tf_op | source)
XLA Modules:
  0.0 529.3 jit_solution(9411245141174349664)
XLA Ops:
  12.3 49.0 %all-gather.12.cloned.1.call-done = bf16[1024,896]{0,1:T(8,128)(2,1)} async-done(((bf16[128,896]{0,1:T(8,128)(2,1)}), bf16[1024,896]{0,1:T(8,128)(2,1)}) %all-gather.12.cloned.1.call-update) | async-done | bytes 1835024 | tf_op jit(solution)/shard_map/all_gather | solution.py:184
  62.2 22.8 %all-gather.10.cloned.1.call-done = bf16[512,2176]{1,0:T(8,128)(2,1)} async-done(((bf16[128,2176]{1,0:T(8,128)(2,1)}), bf16[512,2176]{1,0:T(8,128)(2,1)}) %all-gather.10.cloned.1.call-update) | async-done | bytes 2228240 | tf_op jit(solution)/shard_map/all_gather | solution.py:177
  92.7 23.9 %all_to_all.35.qkv_ref = bf16[4,224,512]{2,1,0:T(8,128)(2,1)S(1)} all-to-all(bf16[4,224,512]{2,1,0:T(8,128)(2,1)S(1)} %constant_dynamic-update-slice_fusion), channel_id=1, replica_groups={{0,4,8,12},{16,20,24,28},{1,5,9,13},{17,21,25,29},{2,6,10,14},{18,22,26..., dimensions={0} | all-to-all | bytes 1835008 | tf_op jit(solution)/shard_map/all_to_all | solution.py:158
  116.6 7.8 %attend.1 = (bf16[4,64,512]{2,1,0:T(8,128)(2,1)S(1)}, f32[4,64,512]{2,1,0:T(8,128)S(1)}, f32[4,1,512]{2,1,0:T(1,128)S(1)}) custom-call(bf16[4,224,512]{2,1,0:T(8,128)(2,1)S(1)} %all_to_all.35.qkv_ref), custom_call_target="tpu_custom_call" | custom-call | flops 2147483648 | bytes 2097152 | tf_op jit(solution)/shard_map/attend/pallas_call | solution.py:72
  124.4 11.5 %all_to_all.36 = bf16[4,64,512]{2,1,0:T(8,128)(2,1)} all-to-all(bf16[4,64,512]{2,1,0:T(8,128)(2,1)S(1)} %get-tuple-element.11), channel_id=1, replica_groups={{0,4,8,12},{16,20,24,28},{1,5,9,13},{17,21,25,29},{2,6,10,14},{18,22,26..., dimensions={0} | all-to-all | bytes 524288 | tf_op jit(solution)/shard_map/all_to_all | solution.py:158
  138.5 6.8 %all-gather.16.cloned.1.call-done = bf16[1024,1024]{1,0:T(8,128)(2,1)} async-done(((bf16[128,1024]{1,0:T(8,128)(2,1)}), bf16[1024,1024]{1,0:T(8,128)(2,1)}) %all-gather.16.cloned.1.call-update) | async-done | bytes 2097168 | tf_op jit(solution)/shard_map/all_gather | solution.py:194
  145.3 17.2 %all-gather.14.cloned.1.call-done = bf16[1024,512]{1,0:T(8,128)(2,1)} async-done(((bf16[256,512]{1,0:T(8,128)(2,1)}), bf16[1024,512]{1,0:T(8,128)(2,1)}) %all-gather.14.cloned.1.call-update) | async-done | bytes 1048592 | tf_op jit(solution)/shard_map/all_gather | solution.py:240
  169.0 77.1 %all-gather.18.cloned.1.call-done = bf16[1024,2304]{0,1:T(8,128)(2,1)} async-done(((bf16[128,2304]{0,1:T(8,128)(2,1)}), bf16[1024,2304]{0,1:T(8,128)(2,1)}) %all-gather.18.cloned.1.call-update) | async-done | bytes 4718608 | tf_op jit(solution)/shard_map/all_gather | solution.py:195
  246.1 4.5 fusion.2
  250.6 4.2 fusion.12
  261.4 14.1 %all-to-all-done.3 = bf16[4,128,1024]{2,1,0:T(8,128)(2,1)S(1)} async-done(((bf16[4,128,1024]{2,1,0:T(8,128)(2,1)}), bf16[4,128,1024]{2,1,0:T(8,128)(2,1)S(1)}, u32[]{:S(2)}, u32[]{:S(2)}) %all-to-all-start.3) | async-done | bytes 1048608 | tf_op jit(solution)/shard_map/all_to_all | solution.py:166
  279.3 3.6 convolution_convert_fusion.2
  282.9 3.6 convolution_convert_fusion
  286.5 6.9 %all-gather.20.cloned.1.call-done = bf16[512,1024]{1,0:T(8,128)(2,1)} async-done(((bf16[128,1024]{1,0:T(8,128)(2,1)}), bf16[512,1024]{1,0:T(8,128)(2,1)}) %all-gather.20.cloned.1.call-update) | async-done | bytes 1048592 | tf_op jit(solution)/shard_map/all_gather | solution.py:260
  294.9 4.8 pad_maximum_fusion
  302.5 16.3 %all_to_all.37.grad_ref = bf16[4,64,512]{2,1,0:T(8,128)(2,1)S(1)} all-to-all(bf16[4,64,512]{2,1,0:T(8,128)(2,1)S(1)} %bitcast.125), channel_id=1, replica_groups={{0,4,8,12},{16,20,24,28},{1,5,9,13},{17,21,25,29},{2,6,10,14},{18,22,26..., dimensions={0} | all-to-all | bytes 524288 | tf_op jit(solution)/shard_map/all_to_all | solution.py:158
  318.7 13.6 %attend_back.1 = bf16[4,192,512]{2,1,0:T(8,128)(2,1)} custom-call(bf16[4,224,512]{2,1,0:T(8,128)(2,1)S(1)} %all_to_all.35.qkv_ref, bf16[4,64,512]{2,1,0:T(8,128)(2,1)S(1)} %all_to_all.37.grad_ref, f32[4,64,512]{2,1,0:T(8,128)S(1)} %get-tuple-element.12.wide_ref, f32[4,1,512]{2,1,0:T(1,128)S(1)} %get-tuple-element.13.lse_ref), custom_call_target="tpu_custom_call" | custom-call | flops 5368709120 | bytes 3145728 | tf_op jit(solution)/shard_map/attend_back/pallas_call | solution.py:126
  335.9 26.1 %all-to-all-done.5 = bf16[4,192,512]{2,1,0:T(8,128)(2,1)S(1)} async-done(((bf16[4,192,512]{2,1,0:T(8,128)(2,1)}), bf16[4,192,512]{2,1,0:T(8,128)(2,1)S(1)}, u32[]{:S(2)}, u32[]{:S(2)}) %all-to-all-start.5) | async-done | bytes 786464 | tf_op jit(solution)/shard_map/all_to_all | solution.py:158
  371.3 42.3 %reduce-scatter.5.cloned.1.call-done = bf16[128,2560]{1,0:T(8,128)(2,1)} async-done(((bf16[1024,2560]{1,0:T(8,128)(2,1)}), bf16[128,2560]{1,0:T(8,128)(2,1)}) %reduce-scatter.5.cloned.1.call-update) | async-done | bytes 655376 | tf_op jit(solution)/shard_map/reduce_scatter | solution.py:269
  416.0 17.0 %all_to_all.38 = bf16[4,128,1024]{2,1,0:T(8,128)(2,1)S(1)} all-to-all(bf16[4,128,1024]{2,1,0:T(8,128)(2,1)S(1)} %bitcast.122), channel_id=1, replica_groups=mesh['ctx'=8,'heads'=4] {'heads'}, dimensions={0} | all-to-all | bytes 2097152 | tf_op jit(solution)/shard_map/all_to_all | solution.py:166
  438.7 12.3 %all-to-all-done.6 = bf16[4,128,1024]{2,1,0:T(8,128)(2,1)S(1)} async-done(((bf16[4,128,1024]{2,1,0:T(8,128)(2,1)}), bf16[4,128,1024]{2,1,0:T(8,128)(2,1)S(1)}, u32[]{:S(2)}, u32[]{:S(2)}) %all-to-all-start.6) | async-done | bytes 1048608 | tf_op jit(solution)/shard_map/all_to_all | solution.py:166
  454.4 29.0 %reduce-scatter.7.cloned.1.call-done = bf16[128,896]{1,0:T(8,128)(2,1)} async-done(((bf16[1024,896]{1,0:T(8,128)(2,1)}), bf16[128,896]{1,0:T(8,128)(2,1)}) %reduce-scatter.7.cloned.1.call-update) | async-done | bytes 229392
  484.5 9.5 %all-gather = bf16[512,896]{0,1:T(8,128)(2,1)S(1)} all-gather(bf16[128,896]{0,1:T(8,128)(2,1)S(1)} %copy.71), channel_id=2, replica_groups=mesh['ctx'=8,'heads'=4] {'heads'}, dimensions={0}, use_global_device_ids=true | all-gather | bytes 1146880 | tf_op jit(solution)/shard_map/all_gather | solution.py:301
  499.7 9.8 %all-gather.22.cloned.1.call-done = bf16[512,2560]{1,0:T(8,128)(2,1)} async-done(((bf16[128,2560]{1,0:T(8,128)(2,1)}), bf16[512,2560]{1,0:T(8,128)(2,1)}) %all-gather.22.cloned.1.call-update) | async-done | bytes 2621456 | tf_op jit(solution)/shard_map/all_gather | solution.py:300
  (155 shorter events, 81.1 us)
Async XLA Ops:
  7.2 130.4 %copy-start = (bf16[2624,128]{1,0:T(8,128)(2,1)S(1)}, bf16[2624,128]{1,0:T(8,128)(2,1)}, u32[]{:S(2)}) copy-start(bf16[2624,128]{1,0:T(8,128)(2,1)} %param.17) | copy-start | bytes 2015236
  7.2 54.1 %all-gather.12.cloned.1.call-start = ((), (), s32[]{:S(2)}) async-start(), calls=%async_computation.10 | async-start | bytes 2064384 | tf_op jit(solution)/shard_map/all_gather | solution.py:184
  10.3 74.7 %all-gather.10.cloned.1.call-start = ((), (), s32[]{:S(2)}) async-start(), calls=%async_computation.9 | async-start | bytes 2785280 | tf_op jit(solution)/shard_map/all_gather | solution.py:177
  11.4 133.9 %all-gather.16.cloned.1.call-start = ((), (), s32[]{:S(2)}) async-start(), calls=%async_computation.12 | async-start | bytes 2359296 | tf_op jit(solution)/shard_map/all_gather | solution.py:194
  12.2 150.4 %all-gather.14.cloned.1.call-start = ((), (), s32[]{:S(2)}) async-start(), calls=%async_computation.11 | async-start | bytes 1310720 | tf_op jit(solution)/shard_map/all_gather | solution.py:240
  61.3 28.1 %copy-start.14 = (bf16[1024,896]{0,1:T(8,128)(2,1)S(1)}, bf16[1024,896]{0,1:T(8,128)(2,1)}, u32[]{:S(2)}) copy-start(bf16[1024,896]{0,1:T(8,128)(2,1)} %all-gather.12.cloned.1.call-done) | copy-start | bytes 5505028
  136.0 110.1 %all-gather.18.cloned.1.call-start = ((), (), s32[]{:S(2)}) async-start(), calls=%async_computation.13 | async-start | bytes 5308416 | tf_op jit(solution)/shard_map/all_gather | solution.py:195
  246.1 4.5 copy-start.16
  250.6 4.2 copy-start.4
  257.6 18.0 %all-to-all-start.3 = ((bf16[4,128,1024]{2,1,0:T(8,128)(2,1)}), bf16[4,128,1024]{2,1,0:T(8,128)(2,1)S(1)}, u32[]{:S(2)}, u32[]{:S(2)}) async-start(bf16[4,128,1024]{2,1,0:T(8,128)(2,1)} %bitcast.121), calls=%async_computation.3 | async-start | bytes 2097152 | tf_op jit(solution)/shard_map/all_to_all | solution.py:166
  261.1 32.3 %all-gather.20.cloned.1.call-start = ((), (), s32[]{:S(2)}) async-start(), calls=%async_computation.14 | async-start | bytes 1310720 | tf_op jit(solution)/shard_map/all_gather | solution.py:260
  275.7 3.6 copy-start.17
  279.2 134.4 %reduce-scatter.5.cloned.1.call-start = ((), (), s32[]{:S(2)}) async-start(), calls=%async_computation.15 | async-start | bytes 5898240 | tf_op jit(solution)/shard_map/reduce_scatter | solution.py:269
  279.3 3.6 copy-start.5
  279.3 3.6 copy-start.20
  279.3 3.6 copy-start.22
  282.9 10.5 %copy-start.6 = (bf16[1024,512]{1,0:T(8,128)(2,1)S(1)}, bf16[1024,512]{1,0:T(8,128)(2,1)}, u32[]{:S(2)}) copy-start(bf16[1024,512]{1,0:T(8,128)(2,1)} %all-gather.14.cloned.1.call-done) | copy-start | bytes 3145732
  332.3 29.7 %all-to-all-start.5 = ((bf16[4,192,512]{2,1,0:T(8,128)(2,1)}), bf16[4,192,512]{2,1,0:T(8,128)(2,1)S(1)}, u32[]{:S(2)}, u32[]{:S(2)}) async-start(bf16[4,192,512]{2,1,0:T(8,128)(2,1)} %attend_back.1), calls=%async_computation.5 | async-start | bytes 1572864 | tf_op jit(solution)/shard_map/all_to_all | solution.py:158
  335.9 147.6 %reduce-scatter.7.cloned.1.call-start = ((), (), s32[]{:S(2)}) async-start(), calls=%async_computation.17 | async-start | bytes 2064384
  371.2 42.4 %copy-start.18 = (bf16[512,768]{1,0:T(8,128)(2,1)S(1)}, bf16[512,768]{1,0:T(8,128)(2,1)}, u32[]{:S(2)}) copy-start(bf16[512,768]{1,0:T(8,128)(2,1)} %get-tuple-element.40) | copy-start | bytes 2359300
  371.2 138.2 %all-gather.22.cloned.1.call-start = ((), (), s32[]{:S(2)}) async-start(), calls=%async_computation.16 | async-start | bytes 3276800 | tf_op jit(solution)/shard_map/all_gather | solution.py:300
  433.0 18.0 %all-to-all-start.6 = ((bf16[4,128,1024]{2,1,0:T(8,128)(2,1)}), bf16[4,128,1024]{2,1,0:T(8,128)(2,1)S(1)}, u32[]{:S(2)}, u32[]{:S(2)}) async-start(bf16[4,128,1024]{2,1,0:T(8,128)(2,1)} %bitcast.120), calls=%async_computation.6 | async-start | bytes 2097152 | tf_op jit(solution)/shard_map/all_to_all | solution.py:166
  436.8 15.6 %copy-start.7 = (f32[128,1024]{1,0:T(8,128)S(1)}, f32[128,1024]{1,0:T(8,128)}, u32[]{:S(2)}) copy-start(f32[128,1024]{1,0:T(8,128)} %get-tuple-element.37) | copy-start | bytes 1572868
  519.0 3.8 copy-start.1
  (11 other events, 26.7 us)
Sparse Core Ops, SparseCore 0:
  10.7 50.5 all-gather.11
  63.5 21.5 all-gather.9
  87.1 58.1 all-gather.15
  146.7 15.7 all-gather.13
  165.0 80.9 all-gather.17
  279.3 14.0 all-gather.19
  299.9 113.7 reduce-scatter.4
  417.1 66.3 reduce-scatter.6
  485.1 24.3 all-gather.21

commit v2 on v1

--- a/solution.py
+++ b/solution.py
@@ -27,6 +27,56 @@
     return lax.dot_general(
         left, right, (((left_dim,), (right_dim,)), ((), ())), preferred_element_type=F32
     )
+
+
+def exchange_kernel(count, axis, split, source, target, send, recv, local):
+    place = lax.axis_index(axis)
+    base = place // count * count
+    me = place - base
+    barrier = pltpu.get_barrier_semaphore()
+    for step in range(1, count):
+        peer = lax.rem(me + step, count)
+        pl.semaphore_signal(
+            barrier, inc=1, device_id={axis: base + peer}, device_id_type=pl.DeviceIdType.MESH
+        )
+    pl.semaphore_wait(barrier, count - 1)
+    copies = []
+    for step in range(1, count):
+        peer = lax.rem(me + step, count)
+        copy = pltpu.make_async_remote_copy(
+            src_ref=source.at[peer] if split else source,
+            dst_ref=target.at[me],
+            send_sem=send.at[step - 1],
+            recv_sem=recv.at[step - 1],
+            device_id={axis: base + peer},
+            device_id_type=pl.DeviceIdType.MESH,
+        )
+        copy.start()
+        copies.append(copy)
+    own = pltpu.make_async_copy(source.at[me] if split else source, target.at[me], local)
+    own.start()
+    own.wait()
+    for copy in copies:
+        copy.wait()
+
+
+def exchange(value, axis, count, split, number):
+    shape = value.shape if split else (count, *value.shape)
+    moved = value.size * value.dtype.itemsize * (1 if split else count)
+    return pl.pallas_call(
+        functools.partial(exchange_kernel, count, axis, split),
+        in_specs=[pl.BlockSpec(memory_space=pl.ANY)],
+        out_specs=pl.BlockSpec(memory_space=pl.ANY),
+        out_shape=jax.ShapeDtypeStruct(shape, value.dtype),
+        scratch_shapes=[
+            pltpu.SemaphoreType.DMA((count - 1,)),
+            pltpu.SemaphoreType.DMA((count - 1,)),
+            pltpu.SemaphoreType.DMA,
+        ],
+        compiler_params=pltpu.CompilerParams(collective_id=number, has_side_effects=True),
+        cost_estimate=pl.CostEstimate(flops=0, bytes_accessed=moved * 20, transcendentals=0),
+        name=f"exchange_{number}",
+    )(value)
 
 
 def norm_parts(values):
@@ -140,7 +190,6 @@
 
 def body(tokens, d_out, segment_ids, position_ids, w_qkv, w_attn, w_in, w_out, gain_attn, gain_mlp):
     groups = lax.axis_size("heads")
-    ctx_count = lax.axis_size("ctx")
     member = lax.axis_index("heads")
     rows, width = tokens.shape
     shard = w_qkv.shape[0]
@@ -152,30 +201,26 @@
     hidden = FF // groups
     padded = -(-hidden // 128) * 128
     tile = min(512, block)
-    teams = [[reach * i + j for j in range(reach)] for i in range(ctx_count // reach)]
-
-    def swap(value):
-        return lax.all_to_all(
-            value, "ctx", split_axis=0, concat_axis=0, axis_index_groups=teams, tiled=True
-        )
+
+    def swap(value, number):
+        return exchange(value, "ctx", reach, True, number)
+
+    def heads_gather(value, number):
+        return exchange(value, "heads", groups, False, number)
 
     def own_rows(value):
         return lax.dynamic_slice_in_dim(value, member * rows, rows, 0)
 
-    def heads_sum(value):
-        parts = lax.all_to_all(
-            value.astype(BF).reshape(groups, rows, width),
-            "heads",
-            split_axis=0,
-            concat_axis=0,
-            tiled=True,
+    def heads_sum(value, number):
+        parts = exchange(
+            value.astype(BF).reshape(groups, rows, width), "heads", groups, True, number
         )
         return jnp.sum(parts.astype(F32), axis=0)
 
     extra = jnp.stack([position_ids // 256, position_ids % 256, segment_ids % 2], axis=1)
     extra = jnp.pad(extra.astype(BF), ((0, 0), (0, 125)))
-    gathered_block = lax.all_gather(
-        jnp.concatenate([tokens, d_out, extra], axis=1), "heads", axis=0, tiled=True
+    gathered_block = heads_gather(jnp.concatenate([tokens, d_out, extra], axis=1), 0).reshape(
+        block, 2 * width + 128
     )
     qkv_part = lax.dynamic_slice_in_dim(
         w_qkv.reshape(shard, 3, width), member * lanes, lanes, 2
@@ -234,10 +279,10 @@
         ],
         axis=1,
     ).astype(BF)
-    qkv = swap(outgoing)
+    qkv = swap(outgoing, 1)
     attended, attended_wide, lse = attend(qkv, tile)
-    returned = swap(attended).reshape(lanes, block)
-    attended_all = lax.all_gather(returned, "heads", axis=0, tiled=True)
+    returned = swap(attended, 2).reshape(lanes, block)
+    attended_all = heads_gather(returned, 3).reshape(width, block)
     middle = residual_in + dot(attended_all, full_attn, 0, 0)
     plain_two, inverse_two = norm_parts(middle)
     mlp_input = (plain_two * gain_two).astype(BF)
@@ -251,28 +296,27 @@
     grad_mixed = dot(upstream, out_weights, 1, 0)
     grad_left = grad_mixed * gate_right * (normal_cdf + gate_left * density)
     grad_gate_up = jnp.concatenate([grad_left, grad_mixed * gelu], axis=1).astype(BF)
+    grad_out_part = dot(upstream, mixed, 0, 0)
+    grad_in_part = dot(mlp_input, grad_gate_up, 0, 0)
+    late = lax.psum_scatter(
+        jnp.concatenate([grad_in_part, grad_out_part], axis=1).astype(BF),
+        "ctx",
+        scatter_dimension=0,
+        tiled=True,
+    )
     grad_mlp_part = dot(grad_gate_up, in_weights, 1, 1)
     grad_gain_two = jnp.sum(grad_mlp_part * plain_two, axis=0)
     grad_norm_mid = norm_back(
-        heads_sum(grad_mlp_part), own_rows(plain_two), own_rows(inverse_two), gain_two
+        heads_sum(grad_mlp_part, 4), own_rows(plain_two), own_rows(inverse_two), gain_two
     )
     grad_middle = d_out.astype(F32) + grad_norm_mid
-    grad_branch = lax.all_gather(grad_middle.astype(BF), "heads", axis=0, tiled=True)
+    grad_branch = heads_gather(grad_middle.astype(BF), 5).reshape(block, width)
     attn_rows = lax.dynamic_slice_in_dim(full_attn, member * lanes, lanes, 0)
     grad_attended = dot(attn_rows, grad_branch, 1, 1).astype(BF).reshape(per_group, HD, block)
-    grad_heads = swap(grad_attended)
-    result = (own_rows(middle) + heads_sum(dot(mixed, out_weights, 1, 1))).astype(BF)
-    grad_out_part = dot(upstream, mixed, 0, 0)
-    grad_in_part = dot(mlp_input, grad_gate_up, 0, 0)
+    grad_heads = swap(grad_attended, 6)
     branch_columns = lax.dynamic_slice_in_dim(grad_branch, member * lanes, lanes, 1)
     grad_attn_part = dot(attended_all, branch_columns, 1, 0)
-    late = lax.psum_scatter(
-        jnp.concatenate([grad_in_part, grad_out_part, grad_attn_part], axis=1).astype(BF),
-        "ctx",
-        scatter_dimension=0,
-        tiled=True,
-    )
-    grad_qkv = swap(attend_back(qkv, grad_heads, attended_wide, lse, tile))
+    grad_qkv = swap(attend_back(qkv, grad_heads, attended_wide, lse, tile), 7)
     grad_qkv = grad_qkv.astype(F32).reshape(per_group, 3, 2, HALF, block)
 
     def turn_back(value):
@@ -289,16 +333,18 @@
     grad_qkv_part = dot(attn_input, grad_projected, 0, 1)
     grad_gains = jnp.pad(jnp.stack([grad_gain_one, grad_gain_two], axis=1), ((0, 0), (0, 126)))
     last = lax.psum_scatter(
-        jnp.concatenate([grad_qkv_part, grad_gains], axis=1).astype(BF),
+        jnp.concatenate([grad_qkv_part, grad_gains, grad_attn_part], axis=1).astype(BF),
         "ctx",
         scatter_dimension=0,
         tiled=True,
     )
     grad_input = grad_middle + norm_back(
-        heads_sum(grad_attn_in), own_rows(plain_one), own_rows(inverse_one), gain_one
-    )
-    late_all = lax.all_gather(late, "heads", axis=0)
-    last_all = lax.all_gather(last, "heads", axis=0)
+        heads_sum(grad_attn_in, 8), own_rows(plain_one), own_rows(inverse_one), gain_one
+    )
+    mixed, _ = lax.optimization_barrier((mixed, grad_input))
+    result = (own_rows(middle) + heads_sum(dot(mixed, out_weights, 1, 1), 9)).astype(BF)
+    late_all = heads_gather(late, 10)
+    last_all = heads_gather(last, 11)
     sum_qkv = (
         last_all[:, :, : 3 * lanes]
         .reshape(groups, shard, 3, lanes)
@@ -308,8 +354,8 @@
     )
     gain_sums = jnp.sum(last_all[:, :, 3 * lanes : 3 * lanes + 2].astype(F32), axis=0)
 
-    def columns(start, size):
-        piece = late_all[:, :, start : start + size]
+    def columns(start, size, held=late_all):
+        piece = held[:, :, start : start + size]
         return piece.transpose(1, 0, 2).reshape(shard, groups * size).astype(F32)
 
     sum_in = jnp.concatenate([columns(0, hidden), columns(padded, hidden)], axis=1)
@@ -319,7 +365,7 @@
         .reshape(groups * hidden, shard)
         .astype(F32)
     )
-    sum_attn = columns(3 * padded, lanes)
+    sum_attn = columns(3 * lanes + 128, lanes, last_all)
     return (
         result,
         grad_input,

time: 531 us -> 509 us (0.959)
  Pallas kernels: 21.4 us -> 210 us
  waiting for transfers between devices: 314 us -> 187 us
  blocking collectives: 78.3 us -> 0 us
  starting transfers between devices: 11.1 us -> 0.2 us
  other arithmetic: 30.8 us -> 36.5 us
    pallas_call x0 -> x12, Pallas kernels: none -> 189 us  [exchange(): pl.pallas_call(functools.partial(exchange_kernel, count, axis, split), in...]
    all_to_all x4 -> x0, blocking collectives: 68.7 us -> none  [the longest x3 51.7 us: swap(): lax.all_to_all(value, 'ctx', split_axis=0, concat_axis=0, axis_index_grou...]
    all_gather x4 -> x0, waiting for transfers between devices: 56.7 us -> none  [the longest x1 22.8 us: body(): lax.all_gather(jnp.concatenate([tokens, d_out, extra], axis=1), 'heads',...]
    reduce_scatter x1 -> x2, waiting for transfers between devices: 42.3 us -> 97.3 us  [the longest x1 75.5 us: body(): lax.psum_scatter(jnp.concatenate([grad_in_part, grad_out_part], axis=1).a...]
    all_to_all x3 -> x0, waiting for transfers between devices: 52.5 us -> none  [the longest x2 26.4 us: heads_sum(): lax.all_to_all(value.astype(BF).reshape(groups, rows, width), 'heads', sp...]
    all_gather x1, waiting for transfers between devices: 49 us -> 15 us  [body(): lax.all_gather(jnp.concatenate([qkv_part, gains], axis=1), 'ctx', axis=0,...]
    unnamed x10 -> x5, waiting for transfers between devices: 29.8 us -> 0.76 us
    all_to_all x3 -> x0, starting transfers between devices: 10.6 us -> none  [the longest x2 7.04 us: heads_sum(): lax.all_to_all(value.astype(BF).reshape(groups, rows, width), 'heads', sp...]
  transfers between devices with their start and end apart: 12 -> 5, of which waited for: 12 -> 4; matrix products, arithmetic and copies ran while one was open for 9% -> 8% of each run, Pallas kernels for 4% -> 24%
where the time goes in v2:
time: 509 us; the launch traced here: 507 us
  Pallas kernels  210 us (41%)
  waiting for transfers between devices  187 us (37%)
  other arithmetic  36.5 us (7%)
  matrix products  35.7 us (7%)
  local copies, waits for them, and re-layouts  23.5 us (5%)
  between operations  14.6 us (3%)
    pallas_call x12, Pallas kernels, exchange(): pl.pallas_call(functools.partial(exchange_kernel, count, axis, split), in...  189 us
    reduce_scatter x1, waiting for transfers between devices, body(): lax.psum_scatter(jnp.concatenate([grad_in_part, grad_out_part], axis=1).a...  75.5 us
    all_gather x1, waiting for transfers between devices, body(): lax.all_gather(jnp.concatenate([left_part, right_part, out_part], axis=1)...  74 us
    dot_general x12, matrix products, dot(): lax.dot_general(left, right, (((left_dim,), (right_dim,)), ((), ())), pre...  35.7 us
    reduce_scatter x1, waiting for transfers between devices, body(): lax.psum_scatter(jnp.concatenate([grad_qkv_part, grad_gains, grad_attn_pa...  21.9 us
    all_gather x1, waiting for transfers between devices, body(): lax.all_gather(jnp.concatenate([qkv_part, gains], axis=1), 'ctx', axis=0,...  15 us
    unnamed x82, local copies, waits for them, and re-layouts  13.8 us
    pallas_call x1, Pallas kernels, attend_back(): pl.pallas_call(functools.partial(attend_back_kernel, tile), grid=(count /...  13 us
  transfers between devices with their start and end apart: 5, of which 4 were waited for; matrix products, arithmetic and copies ran while one was open for 8% of the time, Pallas kernels for 24%

profile of v2, /device:TPU:0, one launch (start us, length us, event | category | flops | bytes accessed | tf_op | source)
XLA Modules:
  0.0 507.2 jit_solution(8386995733925987879)
XLA Ops:
  14.7 27.8 %exchange_0.1 = bf16[4,128,2176]{2,1,0:T(8,128)(2,1)} custom-call(bf16[128,2176]{1,0:T(8,128)(2,1)} %fusion.33.source), custom_call_target="tpu_custom_call" | custom-call | bytes 44564480 | tf_op jit(solution)/shard_map/exchange_0/pallas_call | solution.py:66
  46.3 15.0 %all-gather.4.cloned.1.call-done = bf16[1024,896]{0,1:T(8,128)(2,1)} async-done(((bf16[128,896]{0,1:T(8,128)(2,1)}), bf16[1024,896]{0,1:T(8,128)(2,1)}) %all-gather.4.cloned.1.call-update) | async-done | bytes 1835024 | tf_op jit(solution)/shard_map/all_gather | solution.py:229
  66.1 18.8 %exchange_1.1.qkv_ref = bf16[4,224,512]{2,1,0:T(8,128)(2,1)} custom-call(bf16[4,224,512]{2,1,0:T(8,128)(2,1)} %copy-done.18), custom_call_target="tpu_custom_call" | custom-call | bytes 18350080 | tf_op jit(solution)/shard_map/exchange_1/pallas_call | solution.py:66
  86.0 7.8 %attend.1 = (bf16[4,64,512]{2,1,0:T(8,128)(2,1)S(1)}, f32[4,64,512]{2,1,0:T(8,128)S(1)}, f32[4,1,512]{2,1,0:T(1,128)S(1)}) custom-call(bf16[4,224,512]{2,1,0:T(8,128)(2,1)S(1)} %copy-done.2), custom_call_target="tpu_custom_call" | custom-call | flops 2147483648 | bytes 2097152 | tf_op jit(solution)/shard_map/attend/pallas_call | solution.py:122
  94.5 12.1 %exchange_2.1 = bf16[4,64,512]{2,1,0:T(8,128)(2,1)} custom-call(bf16[4,64,512]{2,1,0:T(8,128)(2,1)} %copy-done.6), custom_call_target="tpu_custom_call" | custom-call | bytes 5242880 | tf_op jit(solution)/shard_map/exchange_2/pallas_call | solution.py:66
  106.7 13.7 %exchange_3.1 = bf16[4,256,512]{2,1,0:T(8,128)(2,1)} custom-call(bf16[256,512]{1,0:T(8,128)(2,1)} %bitcast.127), custom_call_target="tpu_custom_call" | custom-call | bytes 20971520 | tf_op jit(solution)/shard_map/exchange_3/pallas_call | solution.py:66
  120.4 3.5 fusion.57
  126.0 74.0 %all-gather.8.cloned.1.call-done = bf16[1024,2304]{0,1:T(8,128)(2,1)} async-done(((bf16[128,2304]{0,1:T(8,128)(2,1)}), bf16[1024,2304]{0,1:T(8,128)(2,1)}) %all-gather.8.cloned.1.call-update) | async-done | bytes 4718608 | tf_op jit(solution)/shard_map/all_gather | solution.py:240
  200.0 4.5 fusion.4
  204.6 4.1 fusion.16
  208.7 3.3 multiply_reduce_fusion
  212.1 13.6 %exchange_4.1 = bf16[4,128,1024]{2,1,0:T(8,128)(2,1)} custom-call(bf16[4,128,1024]{2,1,0:T(8,128)(2,1)} %bitcast.129), custom_call_target="tpu_custom_call" | custom-call | bytes 20971520 | tf_op jit(solution)/shard_map/exchange_4/pallas_call | solution.py:66
  230.5 14.1 %exchange_5.1 = bf16[4,128,1024]{2,1,0:T(8,128)(2,1)} custom-call(bf16[128,1024]{1,0:T(8,128)(2,1)} %get-tuple-element.56.source), custom_call_target="tpu_custom_call" | custom-call | bytes 20971520 | tf_op jit(solution)/shard_map/exchange_5/pallas_call | solution.py:66
  247.2 6.6 %exchange_6.1.grad_ref = bf16[4,64,512]{2,1,0:T(8,128)(2,1)} custom-call(bf16[4,64,512]{2,1,0:T(8,128)(2,1)} %bitcast.132), custom_call_target="tpu_custom_call" | custom-call | bytes 5242880 | tf_op jit(solution)/shard_map/exchange_6/pallas_call | solution.py:66
  254.7 13.0 %attend_back.1.source = bf16[4,192,512]{2,1,0:T(8,128)(2,1)S(1)} custom-call(bf16[4,224,512]{2,1,0:T(8,128)(2,1)S(1)} %copy-done.3, bf16[4,64,512]{2,1,0:T(8,128)(2,1)S(1)} %copy-done.5, f32[4,64,512]{2,1,0:T(8,128)S(1)} %get-tuple-element.13.wide_ref, f32[4,1,512]{2,1,0:T(1,128)S(1)} %get-tuple-element.14.lse_ref), custom_call_target="tpu_custom_call" | custom-call | flops 5368709120 | bytes 3145728 | tf_op jit(solution)/shard_map/attend_back/pallas_call | solution.py:176
  268.6 12.4 %exchange_7.1 = bf16[4,192,512]{2,1,0:T(8,128)(2,1)} custom-call(bf16[4,192,512]{2,1,0:T(8,128)(2,1)} %copy-done.4), custom_call_target="tpu_custom_call" | custom-call | bytes 15728640 | tf_op jit(solution)/shard_map/exchange_7/pallas_call | solution.py:66
  292.8 3.0 fusion.9
  303.8 12.8 %exchange_8.1 = bf16[4,128,1024]{2,1,0:T(8,128)(2,1)} custom-call(bf16[4,128,1024]{2,1,0:T(8,128)(2,1)} %bitcast.128), custom_call_target="tpu_custom_call" | custom-call | bytes 20971520 | tf_op jit(solution)/shard_map/exchange_8/pallas_call | solution.py:66
  321.4 3.4 convolution_convert_fusion.3
  324.8 14.3 %exchange_9.1 = bf16[4,128,1024]{2,1,0:T(8,128)(2,1)} custom-call(bf16[4,128,1024]{2,1,0:T(8,128)(2,1)} %bitcast.130), custom_call_target="tpu_custom_call" | custom-call | bytes 20971520 | tf_op jit(solution)/shard_map/exchange_9/pallas_call | solution.py:66
  341.4 21.9 %reduce-scatter.3.cloned.1.call-done.source = bf16[128,1152]{1,0:T(8,128)(2,1)} async-done(((bf16[1024,1152]{1,0:T(8,128)(2,1)}), bf16[128,1152]{1,0:T(8,128)(2,1)}) %reduce-scatter.3.cloned.1.call-update) | async-done | bytes 294928 | tf_op jit(solution)/shard_map/reduce_scatter | solution.py:335
  363.2 15.0 %exchange_11.1 = bf16[4,128,1152]{2,1,0:T(8,128)(2,1)} custom-call(bf16[128,1152]{1,0:T(8,128)(2,1)} %reduce-scatter.3.cloned.1.call-done.source), custom_call_target="tpu_custom_call" | custom-call | bytes 23592960 | tf_op jit(solution)/shard_map/exchange_11/pallas_call | solution.py:66
  385.6 75.5 %reduce-scatter.5.cloned.1.call-done.source = bf16[128,2304]{1,0:T(8,128)(2,1)} async-done(((bf16[1024,2304]{1,0:T(8,128)(2,1)}), bf16[128,2304]{1,0:T(8,128)(2,1)}) %reduce-scatter.5.cloned.1.call-update) | async-done | bytes 589840 | tf_op jit(solution)/shard_map/reduce_scatter | solution.py:301
  461.1 27.7 %exchange_10.1 = bf16[4,128,2304]{2,1,0:T(8,128)(2,1)} custom-call(bf16[128,2304]{1,0:T(8,128)(2,1)} %reduce-scatter.5.cloned.1.call-done.source), custom_call_target="tpu_custom_call" | custom-call | bytes 47185920 | tf_op jit(solution)/shard_map/exchange_10/pallas_call | solution.py:66
  (172 shorter events, 74.8 us)
Async XLA Ops:
  7.2 5.5 %copy-start = (bf16[2624,128]{1,0:T(8,128)(2,1)S(1)}, bf16[2624,128]{1,0:T(8,128)(2,1)}, u32[]{:S(2)}) copy-start(bf16[2624,128]{1,0:T(8,128)(2,1)} %param.17) | copy-start | bytes 2015236
  7.2 54.1 %all-gather.4.cloned.1.call-start = ((), (), s32[]{:S(2)}) async-start(), calls=%async_computation.2 | async-start | bytes 2064384 | tf_op jit(solution)/shard_map/all_gather | solution.py:229
  10.2 3.4 copy-start.27
  10.2 3.4 copy-start.28
  10.2 3.6 copy-start.19
  10.2 3.6 copy-start.21
  10.3 110.1 %all-gather.6.cloned.1.call-start = ((), (), s32[]{:S(2)}) async-start(), calls=%async_computation.3 | async-start | bytes 2359296 | tf_op jit(solution)/shard_map/all_gather | solution.py:239
  11.0 189.0 %all-gather.8.cloned.1.call-start = ((), (), s32[]{:S(2)}) async-start(), calls=%async_computation.4 | async-start | bytes 5308416 | tf_op jit(solution)/shard_map/all_gather | solution.py:240
  13.5 349.7 %reduce-scatter.3.cloned.1.call-start = ((), (), s32[]{:S(2)}) async-start(), calls=%async_computation.5 | async-start | bytes 2654208 | tf_op jit(solution)/shard_map/reduce_scatter | solution.py:335
  45.4 19.2 %copy-start.22 = (f32[512]{0:T(512)}, f32[512]{0:T(512)S(1)}, u32[]{:S(2)}) copy-start(f32[512]{0:T(512)S(1)} %broadcast_multiply_fusion.3) | copy-start | bytes 6148
  45.9 18.8 %copy-start.25 = (f32[512]{0:T(512)}, f32[512]{0:T(512)S(1)}, u32[]{:S(2)}) copy-start(f32[512]{0:T(512)S(1)} %add_rsqrt_fusion.1) | copy-start | bytes 6148
  46.3 18.7 %copy-start.14 = (f32[32,512]{1,0:T(8,128)}, f32[32,512]{1,0:T(8,128)S(1)}, u32[]{:S(2)}) copy-start(f32[32,512]{1,0:T(8,128)S(1)} %get-tuple-element.85) | copy-start | bytes 196612
  46.3 18.7 %copy-start.16 = (f32[32,512]{1,0:T(8,128)}, f32[32,512]{1,0:T(8,128)S(1)}, u32[]{:S(2)}) copy-start(f32[32,512]{1,0:T(8,128)S(1)} %get-tuple-element.86) | copy-start | bytes 196612
  200.0 4.5 copy-start.30
  204.5 4.2 copy-start.10
  208.7 3.4 copy-start.33
  208.7 3.4 copy-start.35
  212.1 16.3 %copy-start.20 = (bf16[128,1024]{1,0:T(8,128)(2,1)S(1)}, bf16[128,1024]{1,0:T(8,128)(2,1)}, u32[]{:S(2)}) copy-start(bf16[128,1024]{1,0:T(8,128)(2,1)} %param.11) | copy-start | bytes 786436
  230.5 23.2 %copy-start.3 = (bf16[4,224,512]{2,1,0:T(8,128)(2,1)S(1)}, bf16[4,224,512]{2,1,0:T(8,128)(2,1)}, u32[]{:S(2)}) copy-start(bf16[4,224,512]{2,1,0:T(8,128)(2,1)} %exchange_1.1.qkv_ref) | copy-start | bytes 2752516
  268.6 14.7 %copy-start.9 = (bf16[4,256,512]{2,1,0:T(8,128)(2,1)S(1)}, bf16[4,256,512]{2,1,0:T(8,128)(2,1)}, u32[]{:S(2)}) copy-start(bf16[4,256,512]{2,1,0:T(8,128)(2,1)} %exchange_3.1) | copy-start | bytes 3145732
  295.8 165.3 %reduce-scatter.5.cloned.1.call-start = ((), (), s32[]{:S(2)}) async-start(), calls=%async_computation.6 | async-start | bytes 5308416 | tf_op jit(solution)/shard_map/reduce_scatter | solution.py:301
  303.8 15.6 %copy-start.12 = (f32[128,1024]{1,0:T(8,128)S(1)}, f32[128,1024]{1,0:T(8,128)}, u32[]{:S(2)}) copy-start(f32[128,1024]{1,0:T(8,128)} %get-tuple-element.57) | copy-start | bytes 1572868
  316.6 4.8 copy-start.32
  495.5 5.2 %copy-start.1 = (bf16[2624,128]{1,0:T(8,128)(2,1)S(1)}, bf16[2624,128]{1,0:T(8,128)(2,1)}, u32[]{:S(2)}) copy-start(bf16[2624,128]{1,0:T(8,128)(2,1)} %param.17) | copy-start | bytes 2015236
  (18 other events, 33.4 us)
Sparse Core Ops, SparseCore 0:
  10.6 50.5 all-gather.3
  63.4 54.4 all-gather.5
  120.5 79.4 all-gather.7
  295.9 67.2 reduce-scatter.2
  366.7 94.2 reduce-scatter.4

commit v3 on v2

--- a/solution.py
+++ b/solution.py
@@ -74,7 +74,7 @@
             pltpu.SemaphoreType.DMA,
         ],
         compiler_params=pltpu.CompilerParams(collective_id=number, has_side_effects=True),
-        cost_estimate=pl.CostEstimate(flops=0, bytes_accessed=moved * 20, transcendentals=0),
+        cost_estimate=pl.CostEstimate(flops=0, bytes_accessed=moved, transcendentals=0),
         name=f"exchange_{number}",
     )(value)
 
@@ -226,8 +226,9 @@
         w_qkv.reshape(shard, 3, width), member * lanes, lanes, 2
     ).reshape(shard, 3 * lanes)
     gains = jnp.pad(jnp.stack([gain_attn, gain_mlp], axis=1), ((0, 0), (0, 126)))
+    attn_part = lax.dynamic_slice_in_dim(w_attn, member * lanes, lanes, 1)
     first_weights = lax.all_gather(
-        jnp.concatenate([qkv_part, gains], axis=1), "ctx", axis=0, tiled=True
+        jnp.concatenate([qkv_part, gains, attn_part], axis=1), "ctx", axis=0, tiled=True
     )
 
     def fit(value):
@@ -236,7 +237,11 @@
     left_part = fit(lax.dynamic_slice_in_dim(w_in, member * hidden, hidden, 1))
     right_part = fit(lax.dynamic_slice_in_dim(w_in, FF + member * hidden, hidden, 1))
     out_part = fit(lax.dynamic_slice_in_dim(w_out, member * hidden, hidden, 0).T)
-    full_attn = lax.all_gather(w_attn, "ctx", axis=0, tiled=True)
+    full_attn = (
+        heads_gather(first_weights[:, 3 * lanes + 128 :], 12)
+        .transpose(1, 0, 2)
+        .reshape(width, width)
+    )
     mlp_weights = lax.all_gather(
         jnp.concatenate([left_part, right_part, out_part], axis=1), "ctx", axis=0, tiled=True
     )
@@ -332,8 +337,10 @@
     grad_gain_one = jnp.sum(grad_attn_in * plain_one, axis=0)
     grad_qkv_part = dot(attn_input, grad_projected, 0, 1)
     grad_gains = jnp.pad(jnp.stack([grad_gain_one, grad_gain_two], axis=1), ((0, 0), (0, 126)))
+    last_terms = jnp.concatenate([grad_qkv_part, grad_gains, grad_attn_part], axis=1).astype(BF)
+    late, last_terms = lax.optimization_barrier((late, last_terms))
     last = lax.psum_scatter(
-        jnp.concatenate([grad_qkv_part, grad_gains, grad_attn_part], axis=1).astype(BF),
+        last_terms,
         "ctx",
         scatter_dimension=0,
         tiled=True,

time: 509 us -> 384 us (0.75)
  waiting for transfers between devices: 187 us -> 24.6 us
  Pallas kernels: 210 us -> 238 us
  local copies, waits for them, and re-layouts: 23.5 us -> 31.9 us
    all_gather x1, waiting for transfers between devices: 74 us -> 0.01 us  [body(): lax.all_gather(jnp.concatenate([left_part, right_part, out_part], axis=1)...]
    reduce_scatter x1, waiting for transfers between devices: 75.5 us -> 5 us  [body(): lax.psum_scatter(jnp.concatenate([grad_in_part, grad_out_part], axis=1).a...]
    pallas_call x12 -> x13, Pallas kernels: 189 us -> 217 us  [exchange(): pl.pallas_call(functools.partial(exchange_kernel, count, axis, split), in...]
    reduce_scatter x1, waiting for transfers between devices: 21.9 us -> 0.01 us  [body(): last = lax.psum_scatter(last_terms, 'ctx', scatter_dimension=0, tiled=True)]
    all_gather x2 -> x1, waiting for transfers between devices: 15 us -> 19.6 us  [body(): lax.all_gather(jnp.concatenate([qkv_part, gains, attn_part], axis=1), 'ct...]
    unnamed x82 -> x80, local copies, waits for them, and re-layouts: 13.8 us -> 14.7 us
  transfers between devices with their start and end apart: 5 -> 4, of which waited for: 4 -> 2; matrix products, arithmetic and copies ran while one was open for 8% -> 19% of each run, Pallas kernels for 24% -> 58%
where the time goes in v3:
time: 384 us; the launch traced here: 382 us
  Pallas kernels  238 us (62%)
  matrix products  37.2 us (10%)
  other arithmetic  35.8 us (9%)
  local copies, waits for them, and re-layouts  31.9 us (8%)
  waiting for transfers between devices  24.6 us (6%)
  between operations  14.6 us (4%)
    pallas_call x13, Pallas kernels, exchange(): pl.pallas_call(functools.partial(exchange_kernel, count, axis, split), in...  217 us
    dot_general x12, matrix products, dot(): lax.dot_general(left, right, (((left_dim,), (right_dim,)), ((), ())), pre...  37.2 us
    all_gather x1, waiting for transfers between devices, body(): lax.all_gather(jnp.concatenate([qkv_part, gains, attn_part], axis=1), 'ct...  19.6 us
    unnamed x80, local copies, waits for them, and re-layouts  14.7 us
    pallas_call x1, Pallas kernels, attend_back(): pl.pallas_call(functools.partial(attend_back_kernel, tile), grid=(count /...  12.7 us
    pallas_call x1, Pallas kernels, attend(): pl.pallas_call(functools.partial(attend_kernel, tile), grid=(count // til...  7.79 us
  transfers between devices with their start and end apart: 4, of which 2 were waited for; matrix products, arithmetic and copies ran while one was open for 19% of the time, Pallas kernels for 58%

profile of v3, /device:TPU:0, one launch (start us, length us, event | category | flops | bytes accessed | tf_op | source)
XLA Modules:
  0.0 381.9 jit_solution(2247263251834736036)
XLA Ops:
  14.5 27.8 %exchange_0.1 = bf16[4,128,2176]{2,1,0:T(8,128)(2,1)} custom-call(bf16[128,2176]{1,0:T(8,128)(2,1)} %fusion.35.source), custom_call_target="tpu_custom_call" | custom-call | bytes 2228224 | tf_op jit(solution)/shard_map/exchange_0/pallas_call | solution.py:66
  46.2 19.6 %all-gather.3.cloned.1.call-done = bf16[1024,1152]{1,0:T(8,128)(2,1)} async-done(((bf16[128,1152]{1,0:T(8,128)(2,1)}), bf16[1024,1152]{1,0:T(8,128)(2,1)}) %all-gather.3.cloned.1.call-update) | async-done | bytes 2359312 | tf_op jit(solution)/shard_map/all_gather | solution.py:230
  71.1 16.9 %exchange_1.1.qkv_ref = bf16[4,224,512]{2,1,0:T(8,128)(2,1)} custom-call(bf16[4,224,512]{2,1,0:T(8,128)(2,1)} %copy-done.17), custom_call_target="tpu_custom_call" | custom-call | bytes 917504 | tf_op jit(solution)/shard_map/exchange_1/pallas_call | solution.py:66
  89.1 7.8 %attend.1 = (bf16[4,64,512]{2,1,0:T(8,128)(2,1)S(1)}, f32[4,64,512]{2,1,0:T(8,128)S(1)}, f32[4,1,512]{2,1,0:T(1,128)S(1)}) custom-call(bf16[4,224,512]{2,1,0:T(8,128)(2,1)S(1)} %copy-done.2), custom_call_target="tpu_custom_call" | custom-call | flops 2147483648 | bytes 2097152 | tf_op jit(solution)/shard_map/attend/pallas_call | solution.py:122
  97.7 10.2 %exchange_2.1 = bf16[4,64,512]{2,1,0:T(8,128)(2,1)} custom-call(bf16[4,64,512]{2,1,0:T(8,128)(2,1)} %copy-done.6), custom_call_target="tpu_custom_call" | custom-call | bytes 262144 | tf_op jit(solution)/shard_map/exchange_2/pallas_call | solution.py:66
  107.9 13.7 %exchange_3.1 = bf16[4,256,512]{2,1,0:T(8,128)(2,1)} custom-call(bf16[256,512]{1,0:T(8,128)(2,1)} %bitcast.130), custom_call_target="tpu_custom_call" | custom-call | bytes 1048576 | tf_op jit(solution)/shard_map/exchange_3/pallas_call | solution.py:66
  123.5 25.6 %exchange_12.1 = bf16[4,1024,256]{2,1,0:T(8,128)(2,1)} custom-call(bf16[1024,256]{1,0:T(8,128)(2,1)} %slice.163.source), custom_call_target="tpu_custom_call" | custom-call | bytes 2097152 | tf_op jit(solution)/shard_map/exchange_12/pallas_call | solution.py:66
  149.1 4.0 %copy.119 = bf16[1024,4,256]{0,2,1:T(8,128)(2,1)} copy(bf16[1024,4,256]{2,0,1:T(8,128)(2,1)} %bitcast.111) | data formatting | bytes 4194304 | tf_op jit(solution)/shard_map/transpose | solution.py:242
  153.0 3.5 fusion.58
  158.6 4.5 %fusion.4 = f32[512,1536]{1,0:T(8,128)S(1)} fusion(bf16[1024,2304]{0,1:T(8,128)(2,1)} %all-gather.5.cloned.1.call-done, f32[512,1024]{1,0:T(8,128)} %subtract_multiply_fusion, f32[1024]{0:T(1024)S(1)} %get-tuple-element.52), kind=kOutput, calls=%fused_computation.11 | convolution fusion | flops 1611661312 | bytes 8392704 | tf_op jit(solution)/shard_map/dot_general | solution.py:27
  173.1 6.3 %multiply_reduce_fusion = (bf16[1024]{0:T(1024)(128)(2,1)}, bf16[512,1024]{1,0:T(8,128)(2,1)}) fusion(f32[512,1024]{1,0:T(8,128)} %subtract_multiply_fusion, bf16[1024,2304]{0,1:T(8,128)(2,1)} %all-gather.5.cloned.1.call-done, bf16[512,768]{1,0:T(8,128)(2,1)} %copy-done.35, bf16[512,768]{1,0:T(8,128)(2,1)} %copy-done.34), kind=kOutput, calls=%fused_computation.19 | convolution fusion | flops 1615330304 | bytes 7866368 | tf_op jit(solution)/shard_map/dot_general | solution.py:27
  179.4 14.3 %exchange_4.1 = bf16[4,128,1024]{2,1,0:T(8,128)(2,1)} custom-call(bf16[4,128,1024]{2,1,0:T(8,128)(2,1)} %bitcast.132), custom_call_target="tpu_custom_call" | custom-call | bytes 1048576 | tf_op jit(solution)/shard_map/exchange_4/pallas_call | solution.py:66
  198.6 14.4 %exchange_5.1 = bf16[4,128,1024]{2,1,0:T(8,128)(2,1)} custom-call(bf16[128,1024]{1,0:T(8,128)(2,1)} %get-tuple-element.62.source), custom_call_target="tpu_custom_call" | custom-call | bytes 1048576 | tf_op jit(solution)/shard_map/exchange_5/pallas_call | solution.py:66
  215.6 7.5 %exchange_6.1.grad_ref = bf16[4,64,512]{2,1,0:T(8,128)(2,1)} custom-call(bf16[4,64,512]{2,1,0:T(8,128)(2,1)} %bitcast.135), custom_call_target="tpu_custom_call" | custom-call | bytes 262144 | tf_op jit(solution)/shard_map/exchange_6/pallas_call | solution.py:66
  224.0 12.7 %attend_back.1.source = bf16[4,192,512]{2,1,0:T(8,128)(2,1)S(1)} custom-call(bf16[4,224,512]{2,1,0:T(8,128)(2,1)S(1)} %copy-done.3, bf16[4,64,512]{2,1,0:T(8,128)(2,1)S(1)} %copy-done.5, f32[4,64,512]{2,1,0:T(8,128)S(1)} %get-tuple-element.15.wide_ref, f32[4,1,512]{2,1,0:T(1,128)S(1)} %get-tuple-element.16.lse_ref), custom_call_target="tpu_custom_call" | custom-call | flops 5368709120 | bytes 3145728 | tf_op jit(solution)/shard_map/attend_back/pallas_call | solution.py:176
  237.7 14.9 %exchange_7.1 = bf16[4,192,512]{2,1,0:T(8,128)(2,1)} custom-call(bf16[4,192,512]{2,1,0:T(8,128)(2,1)} %copy-done.4), custom_call_target="tpu_custom_call" | custom-call | bytes 786432 | tf_op jit(solution)/shard_map/exchange_7/pallas_call | solution.py:66
  255.8 4.2 %multiply_reduce_fusion.1 = (bf16[1024]{0:T(1024)(128)(2,1)S(1)}, f32[512,1024]{1,0:T(8,128)}, bf16[512,1024]{1,0:T(8,128)(2,1)}) fusion(f32[512]{0:T(512)S(1)} %copy-done.27, f32[512]{0:T(512)S(1)} %copy-done.24, bf16[512,2176]{1,0:T(8,128)(2,1)} %bitcast.105, bf16[768,512]{1,0:T(8,128)(2,1)S(1)} %bitcast.136, bf16[1024,1152]{1,0:T(8,128)(2,1)S(1)} %copy-done.21), kind=kOutput, calls=%fused_computation.20 | convolution fusion | flops 808451072 | bytes 6559744 | tf_op jit(solution)/shard_map/dot_general | solution.py:27
  266.2 5.0 %reduce-scatter.3.cloned.1.call-done.source = bf16[128,2304]{1,0:T(8,128)(2,1)} async-done(((bf16[1024,2304]{1,0:T(8,128)(2,1)}), bf16[128,2304]{1,0:T(8,128)(2,1)}) %reduce-scatter.3.cloned.1.call-update) | async-done | bytes 589840 | tf_op jit(solution)/shard_map/reduce_scatter | solution.py:306
  271.3 13.4 %exchange_8.1 = bf16[4,128,1024]{2,1,0:T(8,128)(2,1)} custom-call(bf16[4,128,1024]{2,1,0:T(8,128)(2,1)} %bitcast.131), custom_call_target="tpu_custom_call" | custom-call | bytes 1048576 | tf_op jit(solution)/shard_map/exchange_8/pallas_call | solution.py:66
  289.4 3.4 convolution_convert_fusion.3
  292.8 14.4 %exchange_9.1 = bf16[4,128,1024]{2,1,0:T(8,128)(2,1)} custom-call(bf16[4,128,1024]{2,1,0:T(8,128)(2,1)} %bitcast.133), custom_call_target="tpu_custom_call" | custom-call | bytes 1048576 | tf_op jit(solution)/shard_map/exchange_9/pallas_call | solution.py:66
  309.4 28.4 %exchange_10.1 = bf16[4,128,2304]{2,1,0:T(8,128)(2,1)} custom-call(bf16[128,2304]{1,0:T(8,128)(2,1)} %reduce-scatter.3.cloned.1.call-done.source), custom_call_target="tpu_custom_call" | custom-call | bytes 2359296 | tf_op jit(solution)/shard_map/exchange_10/pallas_call | solution.py:66
  348.8 15.7 %exchange_11.1 = bf16[4,128,1152]{2,1,0:T(8,128)(2,1)} custom-call(bf16[128,1152]{1,0:T(8,128)(2,1)} %reduce-scatter.5.cloned.1.call-done.source), custom_call_target="tpu_custom_call" | custom-call | bytes 1179648 | tf_op jit(solution)/shard_map/exchange_11/pallas_call | solution.py:66
  370.3 3.1 copy.133
  (173 shorter events, 76.0 us)
Async XLA Ops:
  7.2 5.3 %copy-start = (bf16[2624,128]{1,0:T(8,128)(2,1)S(1)}, bf16[2624,128]{1,0:T(8,128)(2,1)}, u32[]{:S(2)}) copy-start(bf16[2624,128]{1,0:T(8,128)(2,1)} %param.17) | copy-start | bytes 2015236
  7.2 58.5 %all-gather.3.cloned.1.call-start = ((), (), s32[]{:S(2)}) async-start(), calls=%async_computation.2 | async-start | bytes 2654208 | tf_op jit(solution)/shard_map/all_gather | solution.py:230
  10.0 3.4 copy-start.28
  10.0 3.4 copy-start.29
  10.8 2.9 copy-start.18
  10.8 2.9 copy-start.22
  10.8 147.8 %all-gather.5.cloned.1.call-start = ((), (), s32[]{:S(2)}) async-start(), calls=%async_computation.3 | async-start | bytes 5308416 | tf_op jit(solution)/shard_map/all_gather | solution.py:245
  13.4 257.8 %reduce-scatter.3.cloned.1.call-start = ((), (), s32[]{:S(2)}) async-start(), calls=%async_computation.4 | async-start | bytes 5308416 | tf_op jit(solution)/shard_map/reduce_scatter | solution.py:306
  42.3 3.0 copy-start.7
  45.3 24.4 %copy-start.23 = (f32[512]{0:T(512)}, f32[512]{0:T(512)S(1)}, u32[]{:S(2)}) copy-start(f32[512]{0:T(512)S(1)} %broadcast_multiply_fusion.3) | copy-start | bytes 6148
  45.7 24.0 %copy-start.26 = (f32[512]{0:T(512)}, f32[512]{0:T(512)S(1)}, u32[]{:S(2)}) copy-start(f32[512]{0:T(512)S(1)} %add_rsqrt_fusion.1) | copy-start | bytes 6148
  46.1 23.9 %copy-start.13 = (f32[32,512]{1,0:T(8,128)}, f32[32,512]{1,0:T(8,128)S(1)}, u32[]{:S(2)}) copy-start(f32[32,512]{1,0:T(8,128)S(1)} %get-tuple-element.89) | copy-start | bytes 196612
  46.1 23.9 %copy-start.15 = (f32[32,512]{1,0:T(8,128)}, f32[32,512]{1,0:T(8,128)S(1)}, u32[]{:S(2)}) copy-start(f32[32,512]{1,0:T(8,128)S(1)} %get-tuple-element.90) | copy-start | bytes 196612
  158.6 4.5 %copy-start.8 = (bf16[4,128,2176]{2,1,0:T(8,128)(2,1)S(1)}, bf16[4,128,2176]{2,1,0:T(8,128)(2,1)}, u32[]{:S(2)}) copy-start(bf16[4,128,2176]{2,1,0:T(8,128)(2,1)} %exchange_0.1) | copy-start | bytes 6684676
  172.9 175.9 %reduce-scatter.5.cloned.1.call-start = ((), (), s32[]{:S(2)}) async-start(), calls=%async_computation.5 | async-start | bytes 2654208 | tf_op jit(solution)/shard_map/reduce_scatter | solution.py:342
  179.4 17.1 %copy-start.19 = (bf16[128,1024]{1,0:T(8,128)(2,1)S(1)}, bf16[128,1024]{1,0:T(8,128)(2,1)}, u32[]{:S(2)}) copy-start(bf16[128,1024]{1,0:T(8,128)(2,1)} %param.11) | copy-start | bytes 786436
  198.6 24.5 %copy-start.3 = (bf16[4,224,512]{2,1,0:T(8,128)(2,1)S(1)}, bf16[4,224,512]{2,1,0:T(8,128)(2,1)}, u32[]{:S(2)}) copy-start(bf16[4,224,512]{2,1,0:T(8,128)(2,1)} %exchange_1.1.qkv_ref) | copy-start | bytes 2752516
  255.6 4.5 %copy-start.20 = (bf16[3,4,2,32,512]{4,3,2,1,0:T(8,128)(2,1)}, bf16[3,4,2,32,512]{4,3,2,1,0:T(8,128)(2,1)S(1)}, u32[]{:S(2)}) copy-start(bf16[3,4,2,32,512]{4,3,2,1,0:T(8,128)(2,1)S(1)} %pad_maximum_fusion.4) | copy-start | bytes 2359300
  255.8 4.2 %copy-start.25 = (bf16[1024]{0:T(1024)(128)(2,1)S(1)}, bf16[1024]{0:T(1024)(128)(2,1)}, u32[]{:S(2)}) copy-start(bf16[1024]{0:T(1024)(128)(2,1)} %get-tuple-element.73) | copy-start | bytes 6148
  255.8 4.5 %copy-start.10 = (bf16[4,256,512]{2,1,0:T(8,128)(2,1)S(1)}, bf16[4,256,512]{2,1,0:T(8,128)(2,1)}, u32[]{:S(2)}) copy-start(bf16[4,256,512]{2,1,0:T(8,128)(2,1)} %exchange_3.1) | copy-start | bytes 3145732
  271.3 16.1 %copy-start.11 = (f32[128,1024]{1,0:T(8,128)S(1)}, f32[128,1024]{1,0:T(8,128)}, u32[]{:S(2)}) copy-start(f32[128,1024]{1,0:T(8,128)} %get-tuple-element.63) | copy-start | bytes 1572868
  284.6 4.8 %copy-start.33 = (bf16[512,768]{1,0:T(8,128)(2,1)S(1)}, bf16[512,768]{1,0:T(8,128)(2,1)}, u32[]{:S(2)}) copy-start(bf16[512,768]{1,0:T(8,128)(2,1)} %copy-done.32) | copy-start | bytes 2359300
  370.3 3.1 copy-start.12
  370.3 5.0 %copy-start.1 = (bf16[2624,128]{1,0:T(8,128)(2,1)S(1)}, bf16[2624,128]{1,0:T(8,128)(2,1)}, u32[]{:S(2)}) copy-start(bf16[2624,128]{1,0:T(8,128)(2,1)} %param.17) | copy-start | bytes 2015236
  (16 other events, 24.2 us)
Sparse Core Ops, SparseCore 0:
  10.9 54.7 all-gather.2
  68.3 89.0 all-gather.4
  173.1 98.0 reduce-scatter.2
  274.5 68.5 reduce-scatter.4

commit v4 on v3

--- a/solution.py
+++ b/solution.py
@@ -60,11 +60,51 @@
         copy.wait()
 
 
+def paired_gather_kernel(count, axis, source, target, send, recv, local):
+    me = lax.axis_index(axis)
+    pair = me + 1 - 2 * lax.rem(me, 2)
+    half = count // 2
+    barrier = pltpu.get_barrier_semaphore()
+    for peer in [pair] + [lax.rem(me + 2 * k, count) for k in range(1, half)]:
+        pl.semaphore_signal(
+            barrier, inc=1, device_id={axis: peer}, device_id_type=pl.DeviceIdType.MESH
+        )
+    pl.semaphore_wait(barrier, half)
+
+    def push(piece, place, peer, at):
+        copy = pltpu.make_async_remote_copy(
+            src_ref=piece,
+            dst_ref=target.at[place],
+            send_sem=send.at[at],
+            recv_sem=recv.at[at],
+            device_id={axis: peer},
+            device_id_type=pl.DeviceIdType.MESH,
+        )
+        copy.start()
+        return copy
+
+    far = [push(source, me, lax.rem(me + 2 * k, count), k) for k in range(1, half)]
+    near = [push(source, me, pair, 0)]
+    own = pltpu.make_async_copy(source, target.at[me], local)
+    own.start()
+    for k in range(1, half):
+        far[k - 1].wait_recv()
+        origin = lax.rem(me - 2 * k + count, count)
+        near.append(push(target.at[origin], origin, pair, half - 1 + k))
+    own.wait()
+    for copy in far:
+        copy.wait_send()
+    for copy in near:
+        copy.wait()
+
+
 def exchange(value, axis, count, split, number):
     shape = value.shape if split else (count, *value.shape)
     moved = value.size * value.dtype.itemsize * (1 if split else count)
     return pl.pallas_call(
-        functools.partial(exchange_kernel, count, axis, split),
+        functools.partial(exchange_kernel, count, axis, True)
+        if split
+        else functools.partial(paired_gather_kernel, count, axis),
         in_specs=[pl.BlockSpec(memory_space=pl.ANY)],
         out_specs=pl.BlockSpec(memory_space=pl.ANY),
         out_shape=jax.ShapeDtypeStruct(shape, value.dtype),

time: 384 us -> 370 us (0.964)
  Pallas kernels: 238 us -> 202 us
  waiting for transfers between devices: 24.6 us -> 47.1 us
    pallas_call x13, Pallas kernels: 217 us -> 182 us  [exchange(): pl.pallas_call(functools.partial(exchange_kernel, count, axis, True) if s...]
    all_gather x1, waiting for transfers between devices: 0.01 us -> 9.91 us  [body(): lax.all_gather(jnp.concatenate([left_part, right_part, out_part], axis=1)...]
    all_gather x1, waiting for transfers between devices: 19.6 us -> 26.4 us  [body(): lax.all_gather(jnp.concatenate([qkv_part, gains, attn_part], axis=1), 'ct...]
  transfers between devices with their start and end apart: 4 -> 4, of which waited for: 2 -> 4; matrix products, arithmetic and copies ran while one was open for 19% -> 19% of each run, Pallas kernels for 58% -> 52%
where the time goes in v4:
time: 370 us; the launch traced here: 369 us
  Pallas kernels  202 us (55%)
  waiting for transfers between devices  47.1 us (13%)
  matrix products  37.2 us (10%)
  other arithmetic  35.7 us (10%)
  local copies, waits for them, and re-layouts  31.9 us (9%)
  between operations  14.6 us (4%)
    pallas_call x13, Pallas kernels, exchange(): pl.pallas_call(functools.partial(exchange_kernel, count, axis, True) if s...  182 us
    dot_general x12, matrix products, dot(): lax.dot_general(left, right, (((left_dim,), (right_dim,)), ((), ())), pre...  37.2 us
    all_gather x1, waiting for transfers between devices, body(): lax.all_gather(jnp.concatenate([qkv_part, gains, attn_part], axis=1), 'ct...  26.4 us
    unnamed x80, local copies, waits for them, and re-layouts  14.7 us
    pallas_call x1, Pallas kernels, attend_back(): pl.pallas_call(functools.partial(attend_back_kernel, tile), grid=(count /...  12.7 us
    all_gather x1, waiting for transfers between devices, body(): lax.all_gather(jnp.concatenate([left_part, right_part, out_part], axis=1)...  9.91 us
    reduce_scatter x1, waiting for transfers between devices, body(): lax.psum_scatter(jnp.concatenate([grad_in_part, grad_out_part], axis=1).a...  8.27 us
    pallas_call x1, Pallas kernels, attend(): pl.pallas_call(functools.partial(attend_kernel, tile), grid=(count // til...  7.79 us
  transfers between devices with their start and end apart: 4, of which 4 were waited for; matrix products, arithmetic and copies ran while one was open for 19% of the time, Pallas kernels for 52%

profile of v4, /device:TPU:0, one launch (start us, length us, event | category | flops | bytes accessed | tf_op | source)
XLA Modules:
  0.0 369.0 jit_solution(11765651578579811141)
XLA Ops:
  14.5 21.0 %exchange_0.1 = bf16[4,128,2176]{2,1,0:T(8,128)(2,1)} custom-call(bf16[128,2176]{1,0:T(8,128)(2,1)} %fusion.35.source), custom_call_target="tpu_custom_call" | custom-call | bytes 2228224 | tf_op jit(solution)/shard_map/exchange_0/pallas_call | solution.py:104
  39.4 26.4 %all-gather.3.cloned.1.call-done = bf16[1024,1152]{1,0:T(8,128)(2,1)} async-done(((bf16[128,1152]{1,0:T(8,128)(2,1)}), bf16[1024,1152]{1,0:T(8,128)(2,1)}) %all-gather.3.cloned.1.call-update) | async-done | bytes 2359312 | tf_op jit(solution)/shard_map/all_gather | solution.py:270
  71.1 16.9 %exchange_1.1.qkv_ref = bf16[4,224,512]{2,1,0:T(8,128)(2,1)} custom-call(bf16[4,224,512]{2,1,0:T(8,128)(2,1)} %copy-done.17), custom_call_target="tpu_custom_call" | custom-call | bytes 917504 | tf_op jit(solution)/shard_map/exchange_1/pallas_call | solution.py:104
  89.2 7.8 %attend.1 = (bf16[4,64,512]{2,1,0:T(8,128)(2,1)S(1)}, f32[4,64,512]{2,1,0:T(8,128)S(1)}, f32[4,1,512]{2,1,0:T(1,128)S(1)}) custom-call(bf16[4,224,512]{2,1,0:T(8,128)(2,1)S(1)} %copy-done.2), custom_call_target="tpu_custom_call" | custom-call | flops 2147483648 | bytes 2097152 | tf_op jit(solution)/shard_map/attend/pallas_call | solution.py:162
  97.7 10.2 %exchange_2.1 = bf16[4,64,512]{2,1,0:T(8,128)(2,1)} custom-call(bf16[4,64,512]{2,1,0:T(8,128)(2,1)} %copy-done.6), custom_call_target="tpu_custom_call" | custom-call | bytes 262144 | tf_op jit(solution)/shard_map/exchange_2/pallas_call | solution.py:104
  107.9 10.6 %exchange_3.1 = bf16[4,256,512]{2,1,0:T(8,128)(2,1)} custom-call(bf16[256,512]{1,0:T(8,128)(2,1)} %bitcast.130), custom_call_target="tpu_custom_call" | custom-call | bytes 1048576 | tf_op jit(solution)/shard_map/exchange_3/pallas_call | solution.py:104
  120.4 17.6 %exchange_12.1 = bf16[4,1024,256]{2,1,0:T(8,128)(2,1)} custom-call(bf16[1024,256]{1,0:T(8,128)(2,1)} %slice.163.source), custom_call_target="tpu_custom_call" | custom-call | bytes 2097152 | tf_op jit(solution)/shard_map/exchange_12/pallas_call | solution.py:104
  138.1 4.0 %copy.119 = bf16[1024,4,256]{0,2,1:T(8,128)(2,1)} copy(bf16[1024,4,256]{2,0,1:T(8,128)(2,1)} %bitcast.111) | data formatting | bytes 4194304 | tf_op jit(solution)/shard_map/transpose | solution.py:282
  142.0 3.6 fusion.58
  147.6 9.9 %all-gather.5.cloned.1.call-done = bf16[1024,2304]{0,1:T(8,128)(2,1)} async-done(((bf16[128,2304]{0,1:T(8,128)(2,1)}), bf16[1024,2304]{0,1:T(8,128)(2,1)}) %all-gather.5.cloned.1.call-update) | async-done | bytes 4718608 | tf_op jit(solution)/shard_map/all_gather | solution.py:285
  157.5 4.5 %fusion.4 = f32[512,1536]{1,0:T(8,128)S(1)} fusion(bf16[1024,2304]{0,1:T(8,128)(2,1)} %all-gather.5.cloned.1.call-done, f32[512,1024]{1,0:T(8,128)} %subtract_multiply_fusion, f32[1024]{0:T(1024)S(1)} %get-tuple-element.52), kind=kOutput, calls=%fused_computation.11 | convolution fusion | flops 1611661312 | bytes 8392704 | tf_op jit(solution)/shard_map/dot_general | solution.py:27
  172.0 6.3 %multiply_reduce_fusion = (bf16[1024]{0:T(1024)(128)(2,1)}, bf16[512,1024]{1,0:T(8,128)(2,1)}) fusion(f32[512,1024]{1,0:T(8,128)} %subtract_multiply_fusion, bf16[1024,2304]{0,1:T(8,128)(2,1)} %all-gather.5.cloned.1.call-done, bf16[512,768]{1,0:T(8,128)(2,1)} %copy-done.35, bf16[512,768]{1,0:T(8,128)(2,1)} %copy-done.34), kind=kOutput, calls=%fused_computation.19 | convolution fusion | flops 1615330304 | bytes 7866368 | tf_op jit(solution)/shard_map/dot_general | solution.py:27
  178.4 13.6 %exchange_4.1 = bf16[4,128,1024]{2,1,0:T(8,128)(2,1)} custom-call(bf16[4,128,1024]{2,1,0:T(8,128)(2,1)} %bitcast.132), custom_call_target="tpu_custom_call" | custom-call | bytes 1048576 | tf_op jit(solution)/shard_map/exchange_4/pallas_call | solution.py:104
  196.9 11.2 %exchange_5.1 = bf16[4,128,1024]{2,1,0:T(8,128)(2,1)} custom-call(bf16[128,1024]{1,0:T(8,128)(2,1)} %get-tuple-element.62.source), custom_call_target="tpu_custom_call" | custom-call | bytes 1048576 | tf_op jit(solution)/shard_map/exchange_5/pallas_call | solution.py:104
  210.7 9.1 %exchange_6.1.grad_ref = bf16[4,64,512]{2,1,0:T(8,128)(2,1)} custom-call(bf16[4,64,512]{2,1,0:T(8,128)(2,1)} %bitcast.135), custom_call_target="tpu_custom_call" | custom-call | bytes 262144 | tf_op jit(solution)/shard_map/exchange_6/pallas_call | solution.py:104
  220.7 12.7 %attend_back.1.source = bf16[4,192,512]{2,1,0:T(8,128)(2,1)S(1)} custom-call(bf16[4,224,512]{2,1,0:T(8,128)(2,1)S(1)} %copy-done.3, bf16[4,64,512]{2,1,0:T(8,128)(2,1)S(1)} %copy-done.5, f32[4,64,512]{2,1,0:T(8,128)S(1)} %get-tuple-element.15.wide_ref, f32[4,1,512]{2,1,0:T(1,128)S(1)} %get-tuple-element.16.lse_ref), custom_call_target="tpu_custom_call" | custom-call | flops 5368709120 | bytes 3145728 | tf_op jit(solution)/shard_map/attend_back/pallas_call | solution.py:216
  234.3 11.8 %exchange_7.1 = bf16[4,192,512]{2,1,0:T(8,128)(2,1)} custom-call(bf16[4,192,512]{2,1,0:T(8,128)(2,1)} %copy-done.4), custom_call_target="tpu_custom_call" | custom-call | bytes 786432 | tf_op jit(solution)/shard_map/exchange_7/pallas_call | solution.py:104
  249.4 4.2 %multiply_reduce_fusion.1 = (bf16[1024]{0:T(1024)(128)(2,1)S(1)}, f32[512,1024]{1,0:T(8,128)}, bf16[512,1024]{1,0:T(8,128)(2,1)}) fusion(f32[512]{0:T(512)S(1)} %copy-done.27, f32[512]{0:T(512)S(1)} %copy-done.24, bf16[512,2176]{1,0:T(8,128)(2,1)} %bitcast.105, bf16[768,512]{1,0:T(8,128)(2,1)S(1)} %bitcast.136, bf16[1024,1152]{1,0:T(8,128)(2,1)S(1)} %copy-done.21), kind=kOutput, calls=%fused_computation.20 | convolution fusion | flops 808451072 | bytes 6559744 | tf_op jit(solution)/shard_map/dot_general | solution.py:27
  259.7 8.3 %reduce-scatter.3.cloned.1.call-done.source = bf16[128,2304]{1,0:T(8,128)(2,1)} async-done(((bf16[1024,2304]{1,0:T(8,128)(2,1)}), bf16[128,2304]{1,0:T(8,128)(2,1)}) %reduce-scatter.3.cloned.1.call-update) | async-done | bytes 589840 | tf_op jit(solution)/shard_map/reduce_scatter | solution.py:346
  268.1 13.7 %exchange_8.1 = bf16[4,128,1024]{2,1,0:T(8,128)(2,1)} custom-call(bf16[4,128,1024]{2,1,0:T(8,128)(2,1)} %bitcast.131), custom_call_target="tpu_custom_call" | custom-call | bytes 1048576 | tf_op jit(solution)/shard_map/exchange_8/pallas_call | solution.py:104
  286.5 3.4 convolution_convert_fusion.3
  289.9 14.4 %exchange_9.1 = bf16[4,128,1024]{2,1,0:T(8,128)(2,1)} custom-call(bf16[4,128,1024]{2,1,0:T(8,128)(2,1)} %bitcast.133), custom_call_target="tpu_custom_call" | custom-call | bytes 1048576 | tf_op jit(solution)/shard_map/exchange_9/pallas_call | solution.py:104
  306.5 20.1 %exchange_10.1 = bf16[4,128,2304]{2,1,0:T(8,128)(2,1)} custom-call(bf16[128,2304]{1,0:T(8,128)(2,1)} %reduce-scatter.3.cloned.1.call-done.source), custom_call_target="tpu_custom_call" | custom-call | bytes 2359296 | tf_op jit(solution)/shard_map/exchange_10/pallas_call | solution.py:104
  340.1 11.6 %exchange_11.1 = bf16[4,128,1152]{2,1,0:T(8,128)(2,1)} custom-call(bf16[128,1152]{1,0:T(8,128)(2,1)} %reduce-scatter.5.cloned.1.call-done.source), custom_call_target="tpu_custom_call" | custom-call | bytes 1179648 | tf_op jit(solution)/shard_map/exchange_11/pallas_call | solution.py:104
  (173 shorter events, 81.6 us)
Async XLA Ops:
  7.2 5.3 %copy-start = (bf16[2624,128]{1,0:T(8,128)(2,1)S(1)}, bf16[2624,128]{1,0:T(8,128)(2,1)}, u32[]{:S(2)}) copy-start(bf16[2624,128]{1,0:T(8,128)(2,1)} %param.17) | copy-start | bytes 2015236
  7.2 58.6 %all-gather.3.cloned.1.call-start = ((), (), s32[]{:S(2)}) async-start(), calls=%async_computation.2 | async-start | bytes 2654208 | tf_op jit(solution)/shard_map/all_gather | solution.py:270
  10.0 3.4 copy-start.28
  10.0 3.4 copy-start.29
  10.8 2.9 copy-start.18
  10.8 2.9 copy-start.22
  10.8 146.7 %all-gather.5.cloned.1.call-start = ((), (), s32[]{:S(2)}) async-start(), calls=%async_computation.3 | async-start | bytes 5308416 | tf_op jit(solution)/shard_map/all_gather | solution.py:285
  13.4 254.5 %reduce-scatter.3.cloned.1.call-start = ((), (), s32[]{:S(2)}) async-start(), calls=%async_computation.4 | async-start | bytes 5308416 | tf_op jit(solution)/shard_map/reduce_scatter | solution.py:346
  35.5 3.0 copy-start.7
  38.5 31.2 %copy-start.23 = (f32[512]{0:T(512)}, f32[512]{0:T(512)S(1)}, u32[]{:S(2)}) copy-start(f32[512]{0:T(512)S(1)} %broadcast_multiply_fusion.3) | copy-start | bytes 6148
  39.0 30.7 %copy-start.26 = (f32[512]{0:T(512)}, f32[512]{0:T(512)S(1)}, u32[]{:S(2)}) copy-start(f32[512]{0:T(512)S(1)} %add_rsqrt_fusion.1) | copy-start | bytes 6148
  39.4 30.7 %copy-start.13 = (f32[32,512]{1,0:T(8,128)}, f32[32,512]{1,0:T(8,128)S(1)}, u32[]{:S(2)}) copy-start(f32[32,512]{1,0:T(8,128)S(1)} %get-tuple-element.89) | copy-start | bytes 196612
  39.4 30.7 %copy-start.15 = (f32[32,512]{1,0:T(8,128)}, f32[32,512]{1,0:T(8,128)S(1)}, u32[]{:S(2)}) copy-start(f32[32,512]{1,0:T(8,128)S(1)} %get-tuple-element.90) | copy-start | bytes 196612
  157.5 4.5 %copy-start.8 = (bf16[4,128,2176]{2,1,0:T(8,128)(2,1)S(1)}, bf16[4,128,2176]{2,1,0:T(8,128)(2,1)}, u32[]{:S(2)}) copy-start(bf16[4,128,2176]{2,1,0:T(8,128)(2,1)} %exchange_0.1) | copy-start | bytes 6684676
  171.9 168.2 %reduce-scatter.5.cloned.1.call-start = ((), (), s32[]{:S(2)}) async-start(), calls=%async_computation.5 | async-start | bytes 2654208 | tf_op jit(solution)/shard_map/reduce_scatter | solution.py:382
  178.4 16.4 %copy-start.19 = (bf16[128,1024]{1,0:T(8,128)(2,1)S(1)}, bf16[128,1024]{1,0:T(8,128)(2,1)}, u32[]{:S(2)}) copy-start(bf16[128,1024]{1,0:T(8,128)(2,1)} %param.11) | copy-start | bytes 786436
  196.9 22.9 %copy-start.3 = (bf16[4,224,512]{2,1,0:T(8,128)(2,1)S(1)}, bf16[4,224,512]{2,1,0:T(8,128)(2,1)}, u32[]{:S(2)}) copy-start(bf16[4,224,512]{2,1,0:T(8,128)(2,1)} %exchange_1.1.qkv_ref) | copy-start | bytes 2752516
  249.1 4.5 %copy-start.20 = (bf16[3,4,2,32,512]{4,3,2,1,0:T(8,128)(2,1)}, bf16[3,4,2,32,512]{4,3,2,1,0:T(8,128)(2,1)S(1)}, u32[]{:S(2)}) copy-start(bf16[3,4,2,32,512]{4,3,2,1,0:T(8,128)(2,1)S(1)} %pad_maximum_fusion.4) | copy-start | bytes 2359300
  249.4 4.2 %copy-start.25 = (bf16[1024]{0:T(1024)(128)(2,1)S(1)}, bf16[1024]{0:T(1024)(128)(2,1)}, u32[]{:S(2)}) copy-start(bf16[1024]{0:T(1024)(128)(2,1)} %get-tuple-element.73) | copy-start | bytes 6148
  249.4 4.5 %copy-start.10 = (bf16[4,256,512]{2,1,0:T(8,128)(2,1)S(1)}, bf16[4,256,512]{2,1,0:T(8,128)(2,1)}, u32[]{:S(2)}) copy-start(bf16[4,256,512]{2,1,0:T(8,128)(2,1)} %exchange_3.1) | copy-start | bytes 3145732
  268.1 16.4 %copy-start.11 = (f32[128,1024]{1,0:T(8,128)S(1)}, f32[128,1024]{1,0:T(8,128)}, u32[]{:S(2)}) copy-start(f32[128,1024]{1,0:T(8,128)} %get-tuple-element.63) | copy-start | bytes 1572868
  281.7 4.8 %copy-start.33 = (bf16[512,768]{1,0:T(8,128)(2,1)S(1)}, bf16[512,768]{1,0:T(8,128)(2,1)}, u32[]{:S(2)}) copy-start(bf16[512,768]{1,0:T(8,128)(2,1)} %copy-done.32) | copy-start | bytes 2359300
  357.5 3.1 copy-start.12
  357.5 5.0 %copy-start.1 = (bf16[2624,128]{1,0:T(8,128)(2,1)S(1)}, bf16[2624,128]{1,0:T(8,128)(2,1)}, u32[]{:S(2)}) copy-start(bf16[2624,128]{1,0:T(8,128)(2,1)} %param.17) | copy-start | bytes 2015236
  (16 other events, 24.2 us)
Sparse Core Ops, SparseCore 0:
  10.9 54.7 all-gather.2
  68.4 89.0 all-gather.4
  172.0 95.8 reduce-scatter.2
  271.3 68.7 reduce-scatter.4
